TPU v7x, 32 devices: a whole 2x2x4 slice. The times are simulated.
32 devices in a mesh: grp: 2 (over y), freq: 16 (over z, x, core).
Axes of the slice: x: 2, y: 2, z: 4, core: 2. Of those that a mesh axis runs over, the one named last changes fastest.
Arguments:
- source_field: bfloat16 [4, 16, 512, 256], P('grp', 'freq'), parts along dimension 0, may hold values from -6 to 6
- receiver_field: bfloat16 [4, 16, 512, 256], P('grp', 'freq'), parts along dimension 0, may hold values from -6 to 6
- slowness_slabs: bfloat16 [32, 768, 512], P(('grp', 'freq')), parts along dimension 0, may hold values from 0.3984375 to 1.1953125
- slab_map: int32 [4], P('grp'), parts along dimension 0, may hold values from 0 to 15
- reference_gaps: float32 [4, 3], P('grp'), parts along dimension 0, may hold values from 0.1 to 0.3
- reference_index: int32 [4, 512, 256], P('grp'), parts along dimension 0, may hold values from 0 to 1
- frequency_bins: int32 [16], replicated, may hold values from 10 to 120
- shot_corner: int32 [4], P('grp'), parts along dimension 0, may hold values from 0 to 256
Outputs:
- image: float32 [4, 512, 256, 256], P('grp', 'freq'), parts along dimension 0
There are 2 independent parts, one for each index of `grp`. A program takes and returns all parts, laid end to end along the dimension named above; an argument that names none is the same for every part. Nothing has to cross between parts.
All inputs are finite; a program needn't handle non-finite values.
Results may differ from a plain program's by a relative error of at most 0.014.
Values may be sent and summed in bfloat16 or wider, within the bound.
A program may use at most 128 MiB of HBM per device.

v0:
```python
import functools
import math

import jax
import jax.numpy as jnp
import numpy as np
from jax import lax
from jax.experimental import pallas as pl
from jax.experimental.pallas import tpu as pltpu
from jax.sharding import PartitionSpec as P

LAGS = 256

cell_width = 0.0125
layer_thick = 0.0125
bin_hertz = 0.5
period_bins = 500
slow_base = 0.3
chunk = 16
tile = 256


def spectral_order(length):
    half = length // 2
    return np.concatenate([np.arange(half), [half], np.arange(length - 1, half, -1)])


def parts_of(length):
    steps = np.arange(length, dtype=np.int64)
    phases = np.mod(steps[:, None] * steps[None, :], length).astype(np.float32)
    angles = phases * np.float32(2.0 * math.pi / length)
    scale = np.float32(1.0 / math.sqrt(length))
    return np.cos(angles) * scale, np.sin(angles) * scale


def transform_block(length):
    cosine, sine = parts_of(length)
    return np.block([[cosine, -sine], [sine, cosine]]).astype(jnp.bfloat16)


def transform_pair(length):
    cosine, sine = parts_of(length)
    order = spectral_order(length)
    return (
        np.concatenate([cosine[order], sine[order]], axis=1).astype(jnp.bfloat16),
        np.concatenate([cosine[:, order], sine[:, order]], axis=1).astype(jnp.bfloat16),
    )


def lag_table(frequency_bins, lag_count):
    offsets = jnp.arange(lag_count, dtype=jnp.int32) - lag_count // 2
    cycles = jnp.mod(frequency_bins[:, None] * offsets[None, :], period_bins).astype(jnp.float32)
    angles = cycles * (2.0 * math.pi / period_bins)
    return jnp.stack([jnp.cos(angles), -jnp.sin(angles)]).astype(jnp.bfloat16)


def sin_cos(angle):
    turns = jnp.floor(angle * (2.0 / math.pi) + 0.5)
    rest = angle - turns * 1.5707855224609375
    rest = rest - turns * 1.0804334124e-05
    quarter = turns.astype(jnp.int32)
    square = rest * rest
    sine = rest + rest * square * (
        -1.6666654611e-1 + square * (8.3321608736e-3 + square * -1.9515295891e-4)
    )
    cosine = (
        1.0
        - 0.5 * square
        + square * square
        * (4.166664568298827e-2 + square * (-1.388731625493765e-3 + square * 2.443315711809948e-5))
    )
    odd = (quarter & 1) == 1
    sine_out = jnp.where(odd, cosine, sine)
    cosine_out = jnp.where(odd, sine, cosine)
    sine_out = jnp.where((quarter & 2) == 2, -sine_out, sine_out)
    cosine_out = jnp.where(((quarter + 1) & 2) == 2, -cosine_out, cosine_out)
    return sine_out, cosine_out


def window_kernel(
    devices, bins, gaps, source, receiver, table_f, table_i, table_y, windows, bracket,
    received,
    half, spectrum, shifted_a, shifted_b, shifted_c, returned, refocused, fields, cross,
    pair, part, parts, total, slow,
    pair_sems, scatter_sems, gather_sems, cross_sems,
):
    depths, rows_x, cols_y = bracket.shape
    chips = devices // 2
    me = lax.axis_index("freq")
    grp = lax.axis_index("grp")
    core = lax.rem(me, 2)
    chip = me // 2
    other = 1 - core
    share_rows = rows_x // devices
    signs = (1.0, -1.0)
    middle = rows_x // 2
    tiles = rows_x // tile
    group = max(share_rows, chunk)
    groups = tile // group
    shifted = (shifted_a, shifted_b, shifted_c)
    angular = bins[me].astype(jnp.float32) * (2.0 * math.pi * bin_hertz)
    references = []
    for d in range(depths):
        first = gaps[d, 0]
        second = first + gaps[d, 1]
        third = second + gaps[d, 2]
        references.append((slow_base + first, slow_base + second, slow_base + third))

    def lanes(which):
        return pl.ds(which * cols_y, cols_y)

    def remote(source_ref, target_ref, sems, place):
        return pltpu.make_async_remote_copy(
            src_ref=source_ref, dst_ref=target_ref, send_sem=sems[0], recv_sem=sems[1],
            device_id=(grp, place), device_id_type=pl.DeviceIdType.MESH,
        )

    def hop_to(hop):
        return lax.rem(chip + hop, chips)

    def swap_first(d):
        return remote(
            windows.at[d, other], pair.at[d], (pair_sems.at[d, 0], pair_sems.at[d, 1]),
            chip * 2 + other,
        )

    def scatter(d, hop):
        return remote(
            part.at[d, hop_to(hop)], parts.at[d, hop],
            (scatter_sems.at[d, 0, hop], scatter_sems.at[d, 1, hop]), hop_to(hop) * 2 + core,
        )

    def gather(d, hop):
        return remote(
            total.at[d], slow.at[d, core, chip],
            (gather_sems.at[d, 0, hop], gather_sems.at[d, 1, hop]), hop_to(hop) * 2 + core,
        )

    def swap_last(d):
        return remote(
            slow.at[d, core], slow.at[d, core], (pair_sems.at[d, 2], pair_sems.at[d, 3]),
            chip * 2 + other,
        )

    def send_cross(d, hop):
        to = lax.rem(me + hop, devices)
        return remote(
            cross.at[d, to], received.at[d, me],
            (cross_sems.at[d, 0, hop], cross_sems.at[d, 1, hop]), to,
        )

    def begin_scatter(d):
        swap_first(d).wait()
        part[d] = windows[d, core] + pair[d]

        @pl.loop(1, chips)
        def _(hop):
            scatter(d, hop).start()

    def begin_gather(d):
        @pl.loop(1, chips)
        def _(hop):
            scatter(d, hop).wait()

        summed = part[d, chip]
        for hop in range(1, chips):
            summed = summed + parts[d, hop]
        total[d] = summed
        slow[d, core, chip] = summed

        @pl.loop(1, chips)
        def _(hop):
            gather(d, hop).start()

    def begin_last(d):
        @pl.loop(1, chips)
        def _(hop):
            gather(d, hop).wait()

        swap_last(d).start()

    barrier = pltpu.get_barrier_semaphore()

    @pl.loop(1, devices)
    def _(hop):
        pl.semaphore_signal(
            barrier, inc=1, device_id=(grp, lax.rem(me + hop, devices)),
            device_id_type=pl.DeviceIdType.MESH,
        )

    pl.semaphore_wait(barrier, devices - 1)
    for d in range(depths):
        swap_first(d).start()

    columns = lax.broadcasted_iota(jnp.int32, (chunk, cols_y), 1)
    wave_y = jnp.where(columns < cols_y // 2, columns, cols_y - columns).astype(jnp.float32) * (
        2.0 * math.pi / (cols_y * cell_width)
    )
    squares_y = wave_y * wave_y

    def phases(d, ref, magnitude):
        wave_x = magnitude.astype(jnp.float32) * (2.0 * math.pi / (rows_x * cell_width))
        reach = angular * references[d][ref]
        radicand = reach * reach - (wave_x * wave_x + squares_y)
        depth = jnp.sqrt(jnp.abs(radicand)) * layer_thick
        moving = radicand > 0.0
        fading = jnp.exp(jnp.where(moving, 0.0, -depth))
        sine, cosine = sin_cos(jnp.where(moving, depth, 0.0) - reach * layer_thick)
        return fading * cosine, fading * sine

    def apply_phase(target, cosine, sine, start):
        rows = pl.ds(start, chunk)
        low_rows = pl.ds(rows_x + start, chunk)
        for which in range(2):
            turned = signs[which] * sine
            real = spectrum[rows, lanes(which)]
            imag = spectrum[low_rows, lanes(which)]
            new_real = (cosine * real - turned * imag).astype(jnp.bfloat16)
            target[rows, lanes(which)] = new_real
            target[low_rows, lanes(which)] = (-(cosine * imag + turned * real)).astype(jnp.bfloat16)
            target[pl.ds(2 * rows_x + start, chunk), lanes(which)] = -new_real

    counted = lax.broadcasted_iota(jnp.int32, (chunk, cols_y), 0)

    def shift_chunk(d, ref, target, start):
        cosine, sine = phases(d, ref, counted + start)
        apply_phase(target, cosine, sine, start)
        apply_phase(target, cosine, sine, pl.multiple_of(middle + start, chunk))

    def shift_edge(d, ref, target):
        cosine, sine = phases(d, ref, jnp.where(counted == 0, middle, counted))
        apply_phase(target, cosine, sine, middle)

    def multiply(table, values, rows):
        block = table[rows, :]
        real = jnp.dot(block, values[: 2 * rows_x, :], preferred_element_type=jnp.float32)
        imag = jnp.dot(block, values[rows_x:, :], preferred_element_type=jnp.float32)
        return real, imag

    def slow_rows(d, start):
        if share_rows >= chunk:
            block = start // share_rows
            inner = pl.multiple_of(lax.rem(start, share_rows), chunk)
            return slow[d, block // chips, lax.rem(block, chips), pl.ds(inner, chunk), :].astype(
                jnp.float32
            )
        pieces = []
        for piece in range(chunk // share_rows):
            block = start // share_rows + piece
            pieces.append(
                slow[d, block // chips, lax.rem(block, chips)].astype(jnp.float32)
            )
        return jnp.concatenate(pieces, axis=0)

    def store_cross(d, start, which, values):
        if share_rows >= chunk:
            inner = pl.multiple_of(lax.rem(start, share_rows), chunk)
            cross[d, start // share_rows, which, pl.ds(inner, chunk), :] = values.astype(
                jnp.bfloat16
            )
        else:
            for piece in range(chunk // share_rows):
                cross[d, start // share_rows + piece, which] = values[
                    piece * share_rows : (piece + 1) * share_rows
                ].astype(jnp.bfloat16)

    def mix(d, inside, start):
        local = pl.ds(inside, chunk)
        rows = pl.ds(start, chunk)
        slowness = slow_rows(d, start)
        lower = bracket[d, rows, :] == 0
        slow_low = jnp.where(lower, references[d][0], references[d][1])
        slow_gap = jnp.where(
            lower, references[d][1] - references[d][0], references[d][2] - references[d][1]
        )
        weight = jnp.clip((slowness - slow_low) / slow_gap, 0.0, 1.0)
        sine, cosine = sin_cos((angular * layer_thick) * slowness)
        rounded = []
        for which in range(2):
            mixed = []
            for side in range(2):
                first = refocused[0, which, local, lanes(side)]
                second = refocused[1, which, local, lanes(side)]
                third = refocused[2, which, local, lanes(side)]
                low = jnp.where(lower, first, second)
                high = jnp.where(lower, second, third)
                mixed.append((1.0 - weight) * low + weight * high)
            turned = signs[which] * sine
            real = (cosine * mixed[0] + turned * mixed[1]).astype(jnp.bfloat16)
            imag = (turned * mixed[0] - cosine * mixed[1]).astype(jnp.bfloat16)
            if d < depths - 1:
                fields[which, 0, rows, :] = real
                fields[which, 1, rows, :] = imag
            rounded.append((real.astype(jnp.float32), imag.astype(jnp.float32)))
        (sr, si), (rr, ri) = rounded
        store_cross(d, start, 0, sr * rr + si * ri)
        store_cross(d, start, 1, sr * ri - si * rr)

    for d in range(depths):
        for which, field in enumerate((source, receiver) if d == 0 else (fields.at[0], fields.at[1])):
            for start in range(0, rows_x, tile):
                rows = pl.ds(start, tile)
                both = jnp.concatenate([field[0, rows, :], field[1, rows, :]], axis=1)
                out = jnp.dot(both, table_y[...], preferred_element_type=jnp.float32)
                out = out.astype(jnp.bfloat16)
                half[rows, lanes(which)] = out[:, :cols_y]
                half[pl.ds(rows_x + start, tile), lanes(which)] = out[:, cols_y:]
                half[pl.ds(2 * rows_x + start, tile), lanes(which)] = -out[:, :cols_y]
        if d == 0:
            begin_scatter(0)

        @pl.loop(0, rows_x // tile)
        def _(number):
            start = pl.multiple_of(number * tile, tile)
            real, imag = multiply(table_f, half, pl.ds(start, tile))
            spectrum[pl.ds(start, tile), :] = real
            spectrum[pl.ds(rows_x + start, tile), :] = imag

        if d == 0:
            begin_gather(0)
            for later in range(1, depths):
                begin_scatter(later)

        @pl.loop(0, middle // chunk)
        def _(number):
            shift_chunk(d, 0, shifted[0], pl.multiple_of(number * chunk, chunk))

        shift_edge(d, 0, shifted[0])
        own_tile = me * share_rows // tile
        own_group = lax.rem(me * share_rows, tile) // group
        for turn in range(tiles):
            tile_start = pl.multiple_of(lax.rem(own_tile + 1 + turn, tiles) * tile, tile)
            for ref in range(3):
                if turn == 0 and ref < 2:
                    part_rows = tile // 2

                    @pl.loop(0, 2)
                    def _(side):
                        inner = pl.multiple_of(side * part_rows, part_rows)
                        real, imag = multiply(
                            table_i, shifted[ref], pl.ds(tile_start + inner, part_rows)
                        )
                        returned[pl.ds(inner, part_rows), :] = real.astype(jnp.bfloat16)
                        returned[pl.ds(tile + inner, part_rows), :] = imag.astype(jnp.bfloat16)
                        for each in range(middle // chunk // 2):
                            shift_chunk(
                                d, ref + 1, shifted[ref + 1],
                                pl.multiple_of(side * (middle // 2) + each * chunk, chunk),
                            )

                    shift_edge(d, ref + 1, shifted[ref + 1])
                else:
                    real, imag = multiply(table_i, shifted[ref], pl.ds(tile_start, tile))
                    returned[:tile, :] = real.astype(jnp.bfloat16)
                    returned[tile:, :] = imag.astype(jnp.bfloat16)
                for which in range(2):
                    both = jnp.concatenate(
                        [returned[:tile, lanes(which)], returned[tile:, lanes(which)]], axis=1
                    )
                    refocused[ref, which] = jnp.dot(
                        both, table_y[...], preferred_element_type=jnp.float32
                    )
                if d == 0 and turn == 0 and ref == 0:
                    begin_last(0)
                if d == 0 and turn == 0 and ref == 1:
                    for later in range(1, depths):
                        begin_gather(later)
                if d == 0 and turn == tiles - 1 and ref == 1:
                    for later in range(1, depths):
                        begin_last(later)
            if d == 0 and turn == 0:
                swap_last(0).wait()

            def send_group(index):
                for each in range(group // share_rows):
                    to = (tile_start + index * group) // share_rows + each
                    hop = lax.rem(to - me + devices, devices)

                    @pl.when(hop != 0)
                    def _():
                        send_cross(d, hop).start()

            def turn_index(number):
                return lax.rem(own_group + 1 + number, groups)

            @pl.loop(0, groups)
            def _(number):
                for each in range(group // chunk):
                    inside = pl.multiple_of(turn_index(number) * group + each * chunk, chunk)
                    mix(d, inside, pl.multiple_of(tile_start + inside, chunk))

                @pl.when(number > 0)
                def _():
                    send_group(turn_index(number - 1))

            send_group(turn_index(groups - 1))

        if d == 0:
            for later in range(1, depths):
                swap_last(later).wait()
        received[d, me] = cross[d, me]
    for d in range(depths):
        @pl.loop(1, devices)
        def _(hop):
            send_cross(d, hop).wait()


def cross_spectra(devices, bins, gaps, source, receiver, windows, bracket):
    depths, rows_x, cols_y = bracket.shape
    chips = devices // 2
    share_rows = rows_x // devices
    table_f, table_i = transform_pair(rows_x)
    vmem = pl.BlockSpec(memory_space=pltpu.VMEM)
    flops = 16 * rows_x * (2 * rows_x + 2 * cols_y) * 2 * cols_y * depths
    dma = pltpu.SemaphoreType.DMA
    held = (depths, chips, share_rows, cols_y)
    return pl.pallas_call(
        functools.partial(window_kernel, devices),
        out_shape=jax.ShapeDtypeStruct((depths, devices, 2, share_rows, cols_y), jnp.bfloat16),
        in_specs=[pl.BlockSpec(memory_space=pltpu.SMEM)] * 2 + [vmem] * 7,
        out_specs=vmem,
        scratch_shapes=[
            pltpu.VMEM((3 * rows_x, 2 * cols_y), jnp.bfloat16),
            pltpu.VMEM((2 * rows_x, 2 * cols_y), jnp.float32),
            pltpu.VMEM((3 * rows_x, 2 * cols_y), jnp.bfloat16),
            pltpu.VMEM((3 * rows_x, 2 * cols_y), jnp.bfloat16),
            pltpu.VMEM((3 * rows_x, 2 * cols_y), jnp.bfloat16),
            pltpu.VMEM((2 * tile, 2 * cols_y), jnp.bfloat16),
            pltpu.VMEM((3, 2, tile, 2 * cols_y), jnp.float32),
            pltpu.VMEM((2, 2, rows_x, cols_y), jnp.bfloat16),
            pltpu.VMEM((depths, devices, 2, share_rows, cols_y), jnp.bfloat16),
            pltpu.VMEM(held, jnp.bfloat16),
            pltpu.VMEM(held, jnp.bfloat16),
            pltpu.VMEM(held, jnp.bfloat16),
            pltpu.VMEM((depths, share_rows, cols_y), jnp.bfloat16),
            pltpu.VMEM((depths, 2, chips, share_rows, cols_y), jnp.bfloat16),
            dma((depths, 4)),
            dma((depths, 2, chips)),
            dma((depths, 2, chips)),
            dma((depths, 2, devices)),
        ],
        cost_estimate=pl.CostEstimate(
            flops=4 * flops, bytes_accessed=8 * 1024 * 1024, transcendentals=0
        ),
        compiler_params=pltpu.CompilerParams(
            collective_id=0, has_side_effects=True, vmem_limit_bytes=56 * 1024 * 1024
        ),
    )(
        bins, gaps, source, receiver, jnp.asarray(table_f), jnp.asarray(table_i),
        jnp.asarray(transform_block(cols_y)),
        windows.reshape(depths, 2, chips, share_rows, cols_y), bracket,
    )


def cut_kernel(slab_count, slab_map, corner, slab, out):
    owner = slab_map[pl.program_id(0)] // slab_count
    _, rows_x, cols_y = out.shape
    _, rows_all, cols_all = slab.shape
    held = lax.axis_index("freq")

    @pl.when(owner != held)
    def _():
        out[...] = jnp.zeros(out.shape, out.dtype)

    @pl.when(owner == held)
    def _():
        base = corner[0] // chunk * chunk
        up = lax.rem(2 * chunk - (corner[0] - base), 2 * chunk)
        left = lax.rem(cols_all - corner[1], cols_all)

        @pl.loop(0, rows_x // chunk)
        def _(number):
            start = pl.multiple_of(base + number * chunk, chunk)
            after = pl.multiple_of(jnp.minimum(start + chunk, rows_all - chunk), chunk)
            both = jnp.concatenate(
                [slab[0, pl.ds(start, chunk), :], slab[0, pl.ds(after, chunk), :]], axis=0
            ).astype(jnp.float32)
            both = pltpu.roll(both, up, 0)[:chunk]
            both = pltpu.roll(both, left, 1)[:, :cols_y]
            out[0, pl.ds(pl.multiple_of(number * chunk, chunk), chunk), :] = both.astype(out.dtype)


def cut_windows(slab_map, corner, slabs, rows_x, cols_y):
    slab_count, rows_all, cols_all = slabs.shape
    depths = slab_map.shape[0]
    return pl.pallas_call(
        functools.partial(cut_kernel, slab_count),
        out_shape=jax.ShapeDtypeStruct((depths, rows_x, cols_y), slabs.dtype),
        grid_spec=pltpu.PrefetchScalarGridSpec(
            num_scalar_prefetch=2,
            grid=(depths,),
            in_specs=[
                pl.BlockSpec(
                    (1, rows_all, cols_all),
                    lambda d, slab_map, corner: (lax.rem(slab_map[d], slab_count), 0, 0),
                )
            ],
            out_specs=pl.BlockSpec((1, rows_x, cols_y), lambda d, slab_map, corner: (d, 0, 0)),
        ),
    )(slab_map, corner, slabs)


def image_kernel(scale, crosses, weights, out):
    _, slots, _, rows, cols_y = crosses.shape
    values = crosses[0].astype(jnp.float32).reshape(2 * slots, rows, cols_y)
    values = jnp.swapaxes(values, 0, 1).astype(jnp.bfloat16)
    for row in range(rows):
        out[0, row] = scale * lax.dot_general(
            values[row], weights[...], (((0,), (0,)), ((), ())),
            preferred_element_type=jnp.float32,
        )


def lag_image(crosses, weights):
    depths, slots, _, rows, cols_y = crosses.shape
    lag_count = weights.shape[1]
    step = min(8, rows)
    return pl.pallas_call(
        functools.partial(image_kernel, slots ** (-0.5)),
        out_shape=jax.ShapeDtypeStruct((depths, rows, cols_y, lag_count), jnp.float32),
        grid=(depths, rows // step),
        in_specs=[
            pl.BlockSpec((1, slots, 2, step, cols_y), lambda d, r: (d, 0, 0, r, 0)),
            pl.BlockSpec((2 * slots, lag_count), lambda d, r: (0, 0)),
        ],
        out_specs=pl.BlockSpec((1, step, cols_y, lag_count), lambda d, r: (d, r, 0, 0)),
    )(crosses, weights)


def shards(
    devices,
    source_field,
    receiver_field,
    slowness_slabs,
    slab_map,
    reference_gaps,
    reference_index,
    frequency_bins,
    shot_corner,
):
    rows_x, cols_y = source_field.shape[2:]
    lag_weights = jnp.swapaxes(lag_table(frequency_bins, LAGS), 0, 1)
    windows = cut_windows(slab_map, shot_corner, slowness_slabs, rows_x, cols_y)
    crosses = cross_spectra(
        devices, frequency_bins, reference_gaps, source_field[:, 0], receiver_field[:, 0],
        windows, reference_index,
    )
    return lag_image(crosses, lag_weights.reshape(-1, LAGS))


def solution(mesh):
    placed = (
        P("grp", "freq", None, None),
        P("grp", "freq", None, None),
        P(("grp", "freq"), None, None),
        P("grp"),
        P("grp", None),
        P("grp", None, None),
        P(),
        P("grp"),
    )
    return jax.shard_map(
        functools.partial(shards, mesh.shape["freq"]),
        mesh=mesh,
        in_specs=placed,
        out_specs=P("grp", "freq", None, None),
        check_vma=False,
    )
```

profile of v0, /device:TPU:0, one launch (start us, length us, event | category | flops | bytes accessed | tf_op | source)
XLA Modules:
  0.0 69.3 jit_solution(519067603147439517)
XLA Ops:
  0.0 0.8 %cosine_convert_fusion = (bf16[1,16,256]{2,1,0:T(8,128)(2,1)S(1)}, bf16[1,16,256]{2,1,0:T(8,128)(2,1)S(1)}) fusion(s32[256]{0:T(256)S(1)} %iota_add_fusion, s32[16]{0:T(128)} %bins.1), kind=kLoop, calls=%fused_computation.5 | loop fusion | flops 49152 | bytes 17472 | tf_op jit(solution)/shard_map/convert
  0.8 0.6 reshape.123.weights
  1.5 2.6 %shard_map.109 = bf16[2,512,256]{2,1,0:T(8,128)(2,1)} custom-call(s32[2]{0:T(128)} %slab_map.1, s32[2]{0:T(128)} %corner.1, bf16[1,768,512]{2,1,0:T(8,128)(2,1)} %slab.1), custom_call_target="tpu_custom_call" | custom-call | tf_op jit(solution)/shard_map/pallas_call | solution.py:486
  4.1 56.0 %shard_map.110.crosses = bf16[2,16,2,32,256]{4,3,2,1,0:T(8,128)(2,1)} custom-call(s32[16]{0:T(128)} %bins.1, f32[2,3]{1,0:T(2,128)} %gaps.1, bf16[2,512,256]{2,1,0:T(8,128)(2,1)} %bitcast.6, bf16[2,512,256]{2,1,0:T(8,128)(2,1)} %bitcast.7, bf16[512,1024]{1,0:T(8,128)(2,1)} %constant.23.clone.table_f, bf16[512,1024]{1,0:T(8,128)(2,1)} %constant.24.clone.table_i, ...), custom_call_target="tpu_custom_call" | custom-call | flops 51539607552 | bytes 8388608 | tf_op jit(solution)/shard_map/pallas_call | solution.py:417
  60.1 9.2 %shard_map.111 = f32[2,32,256,256]{3,2,1,0:T(8,128)} custom-call(bf16[2,16,2,32,256]{4,3,2,1,0:T(8,128)(2,1)} %shard_map.110.crosses, bf16[32,256]{1,0:T(8,128)(2,1)} %reshape.123.weights), custom_call_target="tpu_custom_call" | custom-call | tf_op jit(solution)/shard_map/pallas_call | solution.py:518
  (3 shorter events, 0.0 us)
where the time goes:
time: 70.5 us; the launch traced here: 69.3 us
  Pallas kernels  67.8 us (96%)
  other arithmetic  0.81 us (1%)
    pallas_call x1, Pallas kernels, cross_spectra(): pl.pallas_call(functools.partial(window_kernel, devices), out_shape=jax.S...  56 us
    pallas_call x1, Pallas kernels, lag_image(): pl.pallas_call(functools.partial(image_kernel, slots ** (-0.5)), out_shap...  9.21 us
    pallas_call x1, Pallas kernels, cut_windows(): pl.pallas_call(functools.partial(cut_kernel, slab_count), out_shape=jax.S...  2.64 us

commit v1 on v0

--- a/solution.py
+++ b/solution.py
@@ -45,13 +45,6 @@
         np.concatenate([cosine[order], sine[order]], axis=1).astype(jnp.bfloat16),
         np.concatenate([cosine[:, order], sine[:, order]], axis=1).astype(jnp.bfloat16),
     )
-
-
-def lag_table(frequency_bins, lag_count):
-    offsets = jnp.arange(lag_count, dtype=jnp.int32) - lag_count // 2
-    cycles = jnp.mod(frequency_bins[:, None] * offsets[None, :], period_bins).astype(jnp.float32)
-    angles = cycles * (2.0 * math.pi / period_bins)
-    return jnp.stack([jnp.cos(angles), -jnp.sin(angles)]).astype(jnp.bfloat16)
 
 
 def sin_cos(angle):
@@ -78,13 +71,16 @@
 
 
 def window_kernel(
-    devices, bins, gaps, source, receiver, table_f, table_i, table_y, windows, bracket,
-    received,
+    devices, bins, gaps, slab_map, corner, slab_in, source_in, table_y_in, receiver_in,
+    table_f_in, table_i_in, bracket_in,
+    received, weights,
+    slab, source, table_y, receiver, table_f, table_i, bracket,
     half, spectrum, shifted_a, shifted_b, shifted_c, returned, refocused, fields, cross,
-    pair, part, parts, total, slow,
-    pair_sems, scatter_sems, gather_sems, cross_sems,
+    wide, windows, pair, part, parts, total, slow, phase_rows,
+    load_sems, pair_sems, scatter_sems, gather_sems, cross_sems,
 ):
     depths, rows_x, cols_y = bracket.shape
+    slab_count, rows_all, cols_all = slab.shape
     chips = devices // 2
     me = lax.axis_index("freq")
     grp = lax.axis_index("grp")
@@ -106,6 +102,14 @@
         third = second + gaps[d, 2]
         references.append((slow_base + first, slow_base + second, slow_base + third))
 
+    loads = [
+        pltpu.make_async_copy(far, near, load_sems.at[place])
+        for place, (far, near) in enumerate((
+            (slab_in, slab), (source_in, source), (table_y_in, table_y), (receiver_in, receiver),
+            (table_f_in, table_f), (bracket_in, bracket), (table_i_in, table_i),
+        ))
+    ]
+
     def lanes(which):
         return pl.ds(which * cols_y, cols_y)
 
@@ -188,6 +192,51 @@
             device_id_type=pl.DeviceIdType.MESH,
         )
 
+    for load in loads:
+        load.start()
+
+    def one_hot(sizes, offset):
+        ahead = lax.broadcasted_iota(jnp.int32, sizes, 0) - lax.broadcasted_iota(
+            jnp.int32, sizes, 1
+        )
+        return jnp.where(ahead == offset, 1.0, 0.0).astype(jnp.bfloat16)
+
+    def cut_slab(which):
+        pick = one_hot((cols_all, cols_y), corner[1])
+        for start in range(0, rows_all, tile):
+            size = min(tile, rows_all - start)
+            wide[pl.ds(start, size), :] = jnp.dot(
+                slab[which, pl.ds(start, size), :], pick, preferred_element_type=jnp.float32
+            ).astype(jnp.bfloat16)
+
+    def put_windows(steps):
+        kept = []
+        for d in steps:
+            apart = jnp.abs(lax.div(slab_map[d], slab_count) - me)
+            kept.append((1 - jnp.minimum(apart, 1)).astype(jnp.float32))
+        size = max(share_rows, chunk)
+
+        @pl.loop(0, rows_x // size)
+        def _(number):
+            start = number * size
+            pick = one_hot((size, rows_all), -(corner[0] + start))
+            values = jnp.dot(pick, wide[...], preferred_element_type=jnp.float32)
+            for d, keep in zip(steps, kept):
+                held = (values * keep).astype(jnp.bfloat16)
+                for piece in range(size // share_rows):
+                    block = start // share_rows + piece
+                    windows[d, block // chips, lax.rem(block, chips)] = held[
+                        piece * share_rows : (piece + 1) * share_rows
+                    ]
+
+    loads[0].wait()
+    if slab_count == 1:
+        cut_slab(0)
+        put_windows(range(depths))
+    else:
+        for d in range(depths):
+            cut_slab(lax.rem(slab_map[d], slab_count))
+            put_windows((d,))
     pl.semaphore_wait(barrier, devices - 1)
     for d in range(depths):
         swap_first(d).start()
@@ -264,7 +313,7 @@
                     piece * share_rows : (piece + 1) * share_rows
                 ].astype(jnp.bfloat16)
 
-    def mix(d, inside, start):
+    def mix(d, turn, inside, start):
         local = pl.ds(inside, chunk)
         rows = pl.ds(start, chunk)
         slowness = slow_rows(d, start)
@@ -279,9 +328,9 @@
         for which in range(2):
             mixed = []
             for side in range(2):
-                first = refocused[0, which, local, lanes(side)]
-                second = refocused[1, which, local, lanes(side)]
-                third = refocused[2, which, local, lanes(side)]
+                first = refocused[turn, 0, which, local, lanes(side)]
+                second = refocused[turn, 1, which, local, lanes(side)]
+                third = refocused[turn, 2, which, local, lanes(side)]
                 low = jnp.where(lower, first, second)
                 high = jnp.where(lower, second, third)
                 mixed.append((1.0 - weight) * low + weight * high)
@@ -296,19 +345,17 @@
         store_cross(d, start, 0, sr * rr + si * ri)
         store_cross(d, start, 1, sr * ri - si * rr)
 
-    for d in range(depths):
-        for which, field in enumerate((source, receiver) if d == 0 else (fields.at[0], fields.at[1])):
-            for start in range(0, rows_x, tile):
-                rows = pl.ds(start, tile)
-                both = jnp.concatenate([field[0, rows, :], field[1, rows, :]], axis=1)
-                out = jnp.dot(both, table_y[...], preferred_element_type=jnp.float32)
-                out = out.astype(jnp.bfloat16)
-                half[rows, lanes(which)] = out[:, :cols_y]
-                half[pl.ds(rows_x + start, tile), lanes(which)] = out[:, cols_y:]
-                half[pl.ds(2 * rows_x + start, tile), lanes(which)] = -out[:, :cols_y]
-        if d == 0:
-            begin_scatter(0)
-
+    def forward_y(which, field):
+        for start in range(0, rows_x, tile):
+            rows = pl.ds(start, tile)
+            both = jnp.concatenate([field[0, rows, :], field[1, rows, :]], axis=1)
+            out = jnp.dot(both, table_y[...], preferred_element_type=jnp.float32)
+            out = out.astype(jnp.bfloat16)
+            half[rows, lanes(which)] = out[:, :cols_y]
+            half[pl.ds(rows_x + start, tile), lanes(which)] = out[:, cols_y:]
+            half[pl.ds(2 * rows_x + start, tile), lanes(which)] = -out[:, :cols_y]
+
+    def forward_x():
         @pl.loop(0, rows_x // tile)
         def _(number):
             start = pl.multiple_of(number * tile, tile)
@@ -316,88 +363,131 @@
             spectrum[pl.ds(start, tile), :] = real
             spectrum[pl.ds(rows_x + start, tile), :] = imag
 
+    def shift_first(d):
+        @pl.loop(0, middle // chunk)
+        def _(number):
+            shift_chunk(d, 0, shifted[0], pl.multiple_of(number * chunk, chunk))
+
+        shift_edge(d, 0, shifted[0])
+
+    def inverse(d, turn, ref, tile_start):
+        if turn == 0 and ref < 2:
+            part_rows = tile // 2
+
+            @pl.loop(0, 2)
+            def _(side):
+                inner = pl.multiple_of(side * part_rows, part_rows)
+                real, imag = multiply(table_i, shifted[ref], pl.ds(tile_start + inner, part_rows))
+                returned[pl.ds(inner, part_rows), :] = real.astype(jnp.bfloat16)
+                returned[pl.ds(tile + inner, part_rows), :] = imag.astype(jnp.bfloat16)
+                for each in range(middle // chunk // 2):
+                    shift_chunk(
+                        d, ref + 1, shifted[ref + 1],
+                        pl.multiple_of(side * (middle // 2) + each * chunk, chunk),
+                    )
+
+            shift_edge(d, ref + 1, shifted[ref + 1])
+        else:
+            real, imag = multiply(table_i, shifted[ref], pl.ds(tile_start, tile))
+            returned[:tile, :] = real.astype(jnp.bfloat16)
+            returned[tile:, :] = imag.astype(jnp.bfloat16)
+        for which in range(2):
+            both = jnp.concatenate(
+                [returned[:tile, lanes(which)], returned[tile:, lanes(which)]], axis=1
+            )
+            refocused[turn, ref, which] = jnp.dot(
+                both, table_y[...], preferred_element_type=jnp.float32
+            )
+
+    def send_group(d, tile_start, index):
+        for each in range(group // share_rows):
+            to = (tile_start + index * group) // share_rows + each
+            hop = lax.rem(to - me + devices, devices)
+
+            @pl.when(hop != 0)
+            def _():
+                send_cross(d, hop).start()
+
+    own_tile = me * share_rows // tile
+    own_group = lax.rem(me * share_rows, tile) // group
+
+    def turn_index(number):
+        return lax.rem(own_group + 1 + number, groups)
+
+    def mix_tile(d, turn, tile_start):
+        @pl.loop(0, groups)
+        def _(number):
+            for each in range(group // chunk):
+                inside = pl.multiple_of(turn_index(number) * group + each * chunk, chunk)
+                mix(d, turn, inside, pl.multiple_of(tile_start + inside, chunk))
+
+            @pl.when(number > 0)
+            def _():
+                send_group(d, tile_start, turn_index(number - 1))
+
+        send_group(d, tile_start, turn_index(groups - 1))
+
+    def lag_table():
+        lag_count = weights.shape[1]
+        offsets = (
+            lax.broadcasted_iota(jnp.int32, (1, lag_count), 1) - lag_count // 2
+        ).astype(jnp.float32)
+
+        @pl.loop(0, devices)
+        def _(slot):
+            turned = bins[slot].astype(jnp.float32) * offsets
+            phase_rows[pl.ds(2 * slot, 1), :] = turned
+            phase_rows[pl.ds(2 * slot + 1, 1), :] = turned
+
+        counts = phase_rows[...]
+        wraps = jnp.floor((counts + 0.5) * (1.0 / period_bins))
+        sine, cosine = sin_cos((counts - wraps * period_bins) * (2.0 * math.pi / period_bins))
+        odd = lax.broadcasted_iota(jnp.int32, counts.shape, 0) % 2 == 1
+        weights[...] = jnp.where(odd, -sine, cosine).astype(jnp.bfloat16)
+
+    tile_starts = [
+        pl.multiple_of(lax.rem(own_tile + 1 + turn, tiles) * tile, tile) for turn in range(tiles)
+    ]
+    for d in range(depths):
         if d == 0:
+            loads[1].wait()
+            loads[2].wait()
+            forward_y(0, source)
+            begin_scatter(0)
+            loads[3].wait()
+            forward_y(1, receiver)
+            loads[4].wait()
+            forward_x()
+            shift_first(0)
             begin_gather(0)
             for later in range(1, depths):
                 begin_scatter(later)
-
-        @pl.loop(0, middle // chunk)
-        def _(number):
-            shift_chunk(d, 0, shifted[0], pl.multiple_of(number * chunk, chunk))
-
-        shift_edge(d, 0, shifted[0])
-        own_tile = me * share_rows // tile
-        own_group = lax.rem(me * share_rows, tile) // group
-        for turn in range(tiles):
-            tile_start = pl.multiple_of(lax.rem(own_tile + 1 + turn, tiles) * tile, tile)
-            for ref in range(3):
-                if turn == 0 and ref < 2:
-                    part_rows = tile // 2
-
-                    @pl.loop(0, 2)
-                    def _(side):
-                        inner = pl.multiple_of(side * part_rows, part_rows)
-                        real, imag = multiply(
-                            table_i, shifted[ref], pl.ds(tile_start + inner, part_rows)
-                        )
-                        returned[pl.ds(inner, part_rows), :] = real.astype(jnp.bfloat16)
-                        returned[pl.ds(tile + inner, part_rows), :] = imag.astype(jnp.bfloat16)
-                        for each in range(middle // chunk // 2):
-                            shift_chunk(
-                                d, ref + 1, shifted[ref + 1],
-                                pl.multiple_of(side * (middle // 2) + each * chunk, chunk),
-                            )
-
-                    shift_edge(d, ref + 1, shifted[ref + 1])
-                else:
-                    real, imag = multiply(table_i, shifted[ref], pl.ds(tile_start, tile))
-                    returned[:tile, :] = real.astype(jnp.bfloat16)
-                    returned[tile:, :] = imag.astype(jnp.bfloat16)
-                for which in range(2):
-                    both = jnp.concatenate(
-                        [returned[:tile, lanes(which)], returned[tile:, lanes(which)]], axis=1
-                    )
-                    refocused[ref, which] = jnp.dot(
-                        both, table_y[...], preferred_element_type=jnp.float32
-                    )
-                if d == 0 and turn == 0 and ref == 0:
-                    begin_last(0)
-                if d == 0 and turn == 0 and ref == 1:
-                    for later in range(1, depths):
-                        begin_gather(later)
-                if d == 0 and turn == tiles - 1 and ref == 1:
-                    for later in range(1, depths):
-                        begin_last(later)
-            if d == 0 and turn == 0:
-                swap_last(0).wait()
-
-            def send_group(index):
-                for each in range(group // share_rows):
-                    to = (tile_start + index * group) // share_rows + each
-                    hop = lax.rem(to - me + devices, devices)
-
-                    @pl.when(hop != 0)
-                    def _():
-                        send_cross(d, hop).start()
-
-            def turn_index(number):
-                return lax.rem(own_group + 1 + number, groups)
-
-            @pl.loop(0, groups)
-            def _(number):
-                for each in range(group // chunk):
-                    inside = pl.multiple_of(turn_index(number) * group + each * chunk, chunk)
-                    mix(d, inside, pl.multiple_of(tile_start + inside, chunk))
-
-                @pl.when(number > 0)
-                def _():
-                    send_group(turn_index(number - 1))
-
-            send_group(turn_index(groups - 1))
-
-        if d == 0:
+            loads[5].wait()
+            loads[6].wait()
+            for turn in range(tiles):
+                for ref in range(3):
+                    if turn == tiles - 1 and ref == 2:
+                        begin_last(0)
+                        for later in range(1, depths):
+                            begin_gather(later)
+                    inverse(0, turn, ref, tile_starts[turn])
+            lag_table()
+            swap_last(0).wait()
+            for turn in range(tiles):
+                mix_tile(0, turn, tile_starts[turn])
             for later in range(1, depths):
-                swap_last(later).wait()
+                begin_last(later)
+        else:
+            forward_y(0, fields.at[0])
+            forward_y(1, fields.at[1])
+            forward_x()
+            shift_first(d)
+            for turn in range(tiles):
+                for ref in range(3):
+                    inverse(d, turn, ref, tile_starts[turn])
+                if turn == 0:
+                    swap_last(d).wait()
+                mix_tile(d, turn, tile_starts[turn])
         received[d, me] = cross[d, me]
     for d in range(depths):
         @pl.loop(1, devices)
@@ -405,35 +495,55 @@
             send_cross(d, hop).wait()
 
 
-def cross_spectra(devices, bins, gaps, source, receiver, windows, bracket):
+def cross_spectra(
+    devices, bins, gaps, slab_map, corner, source, receiver, slabs, bracket
+):
     depths, rows_x, cols_y = bracket.shape
+    slab_count, rows_all, cols_all = slabs.shape
     chips = devices // 2
     share_rows = rows_x // devices
     table_f, table_i = transform_pair(rows_x)
+    table_y = transform_block(cols_y)
     vmem = pl.BlockSpec(memory_space=pltpu.VMEM)
     flops = 16 * rows_x * (2 * rows_x + 2 * cols_y) * 2 * cols_y * depths
     dma = pltpu.SemaphoreType.DMA
     held = (depths, chips, share_rows, cols_y)
+    field = pltpu.VMEM((2, rows_x, cols_y), jnp.bfloat16)
     return pl.pallas_call(
         functools.partial(window_kernel, devices),
-        out_shape=jax.ShapeDtypeStruct((depths, devices, 2, share_rows, cols_y), jnp.bfloat16),
-        in_specs=[pl.BlockSpec(memory_space=pltpu.SMEM)] * 2 + [vmem] * 7,
-        out_specs=vmem,
+        out_shape=(
+            jax.ShapeDtypeStruct((depths, devices, 2, share_rows, cols_y), jnp.bfloat16),
+            jax.ShapeDtypeStruct((2 * devices, LAGS), jnp.bfloat16),
+        ),
+        in_specs=[pl.BlockSpec(memory_space=pltpu.SMEM)] * 4
+        + [pl.BlockSpec(memory_space=pltpu.HBM)] * 7,
+        out_specs=(vmem, vmem),
         scratch_shapes=[
+            pltpu.VMEM(slabs.shape, jnp.bfloat16),
+            field,
+            pltpu.VMEM(table_y.shape, jnp.bfloat16),
+            field,
+            pltpu.VMEM(table_f.shape, jnp.bfloat16),
+            pltpu.VMEM(table_i.shape, jnp.bfloat16),
+            pltpu.VMEM(bracket.shape, jnp.int32),
             pltpu.VMEM((3 * rows_x, 2 * cols_y), jnp.bfloat16),
             pltpu.VMEM((2 * rows_x, 2 * cols_y), jnp.float32),
             pltpu.VMEM((3 * rows_x, 2 * cols_y), jnp.bfloat16),
             pltpu.VMEM((3 * rows_x, 2 * cols_y), jnp.bfloat16),
             pltpu.VMEM((3 * rows_x, 2 * cols_y), jnp.bfloat16),
             pltpu.VMEM((2 * tile, 2 * cols_y), jnp.bfloat16),
-            pltpu.VMEM((3, 2, tile, 2 * cols_y), jnp.float32),
+            pltpu.VMEM((rows_x // tile, 3, 2, tile, 2 * cols_y), jnp.float32),
             pltpu.VMEM((2, 2, rows_x, cols_y), jnp.bfloat16),
             pltpu.VMEM((depths, devices, 2, share_rows, cols_y), jnp.bfloat16),
+            pltpu.VMEM((rows_all, cols_y), jnp.bfloat16),
+            pltpu.VMEM((depths, 2, chips, share_rows, cols_y), jnp.bfloat16),
             pltpu.VMEM(held, jnp.bfloat16),
             pltpu.VMEM(held, jnp.bfloat16),
             pltpu.VMEM(held, jnp.bfloat16),
             pltpu.VMEM((depths, share_rows, cols_y), jnp.bfloat16),
             pltpu.VMEM((depths, 2, chips, share_rows, cols_y), jnp.bfloat16),
+            pltpu.VMEM((2 * devices, LAGS), jnp.float32),
+            dma((7,)),
             dma((depths, 4)),
             dma((depths, 2, chips)),
             dma((depths, 2, chips)),
@@ -443,66 +553,25 @@
             flops=4 * flops, bytes_accessed=8 * 1024 * 1024, transcendentals=0
         ),
         compiler_params=pltpu.CompilerParams(
-            collective_id=0, has_side_effects=True, vmem_limit_bytes=56 * 1024 * 1024
+            collective_id=0, has_side_effects=True, vmem_limit_bytes=44 * 1024 * 1024
         ),
     )(
-        bins, gaps, source, receiver, jnp.asarray(table_f), jnp.asarray(table_i),
-        jnp.asarray(transform_block(cols_y)),
-        windows.reshape(depths, 2, chips, share_rows, cols_y), bracket,
-    )
-
-
-def cut_kernel(slab_count, slab_map, corner, slab, out):
-    owner = slab_map[pl.program_id(0)] // slab_count
-    _, rows_x, cols_y = out.shape
-    _, rows_all, cols_all = slab.shape
-    held = lax.axis_index("freq")
-
-    @pl.when(owner != held)
-    def _():
-        out[...] = jnp.zeros(out.shape, out.dtype)
-
-    @pl.when(owner == held)
-    def _():
-        base = corner[0] // chunk * chunk
-        up = lax.rem(2 * chunk - (corner[0] - base), 2 * chunk)
-        left = lax.rem(cols_all - corner[1], cols_all)
-
-        @pl.loop(0, rows_x // chunk)
-        def _(number):
-            start = pl.multiple_of(base + number * chunk, chunk)
-            after = pl.multiple_of(jnp.minimum(start + chunk, rows_all - chunk), chunk)
-            both = jnp.concatenate(
-                [slab[0, pl.ds(start, chunk), :], slab[0, pl.ds(after, chunk), :]], axis=0
-            ).astype(jnp.float32)
-            both = pltpu.roll(both, up, 0)[:chunk]
-            both = pltpu.roll(both, left, 1)[:, :cols_y]
-            out[0, pl.ds(pl.multiple_of(number * chunk, chunk), chunk), :] = both.astype(out.dtype)
-
-
-def cut_windows(slab_map, corner, slabs, rows_x, cols_y):
-    slab_count, rows_all, cols_all = slabs.shape
-    depths = slab_map.shape[0]
-    return pl.pallas_call(
-        functools.partial(cut_kernel, slab_count),
-        out_shape=jax.ShapeDtypeStruct((depths, rows_x, cols_y), slabs.dtype),
-        grid_spec=pltpu.PrefetchScalarGridSpec(
-            num_scalar_prefetch=2,
-            grid=(depths,),
-            in_specs=[
-                pl.BlockSpec(
-                    (1, rows_all, cols_all),
-                    lambda d, slab_map, corner: (lax.rem(slab_map[d], slab_count), 0, 0),
-                )
-            ],
-            out_specs=pl.BlockSpec((1, rows_x, cols_y), lambda d, slab_map, corner: (d, 0, 0)),
-        ),
-    )(slab_map, corner, slabs)
+        *[
+            pltpu.with_memory_space_constraint(value, pltpu.HBM)
+            for value in (
+                bins, gaps, slab_map, corner, slabs, source, jnp.asarray(table_y), receiver,
+                jnp.asarray(table_f), jnp.asarray(table_i), bracket,
+            )
+        ]
+    )
 
 
 def image_kernel(scale, crosses, weights, out):
-    _, slots, _, rows, cols_y = crosses.shape
-    values = crosses[0].astype(jnp.float32).reshape(2 * slots, rows, cols_y)
+    _, slots, _, _, cols_y = crosses.shape
+    _, rows, _, _ = out.shape
+    step = pl.multiple_of(pl.program_id(1) * rows, rows)
+    values = crosses[pl.program_id(0), :, :, pl.ds(step, rows), :]
+    values = values.astype(jnp.float32).reshape(2 * slots, rows, cols_y)
     values = jnp.swapaxes(values, 0, 1).astype(jnp.bfloat16)
     for row in range(rows):
         out[0, row] = scale * lax.dot_general(
@@ -515,15 +584,14 @@
     depths, slots, _, rows, cols_y = crosses.shape
     lag_count = weights.shape[1]
     step = min(8, rows)
+    whole = pl.BlockSpec(memory_space=pltpu.VMEM)
     return pl.pallas_call(
         functools.partial(image_kernel, slots ** (-0.5)),
         out_shape=jax.ShapeDtypeStruct((depths, rows, cols_y, lag_count), jnp.float32),
         grid=(depths, rows // step),
-        in_specs=[
-            pl.BlockSpec((1, slots, 2, step, cols_y), lambda d, r: (d, 0, 0, r, 0)),
-            pl.BlockSpec((2 * slots, lag_count), lambda d, r: (0, 0)),
-        ],
+        in_specs=[whole, whole],
         out_specs=pl.BlockSpec((1, step, cols_y, lag_count), lambda d, r: (d, r, 0, 0)),
+        compiler_params=pltpu.CompilerParams(vmem_limit_bytes=24 * 1024 * 1024),
     )(crosses, weights)
 
 
@@ -538,14 +606,11 @@
     frequency_bins,
     shot_corner,
 ):
-    rows_x, cols_y = source_field.shape[2:]
-    lag_weights = jnp.swapaxes(lag_table(frequency_bins, LAGS), 0, 1)
-    windows = cut_windows(slab_map, shot_corner, slowness_slabs, rows_x, cols_y)
-    crosses = cross_spectra(
-        devices, frequency_bins, reference_gaps, source_field[:, 0], receiver_field[:, 0],
-        windows, reference_index,
-    )
-    return lag_image(crosses, lag_weights.reshape(-1, LAGS))
+    crosses, weights = cross_spectra(
+        devices, frequency_bins, reference_gaps, slab_map, shot_corner, source_field[:, 0],
+        receiver_field[:, 0], slowness_slabs, reference_index,
+    )
+    return lag_image(crosses, weights)
 
 
 def solution(mesh):

time: 70.5 us -> 58.2 us (0.83); the launches traced: 69.3 us -> 58 us
  Pallas kernels: 67.8 us -> 58 us
  other arithmetic: 0.81 us -> 0 us
    pallas_call x2 -> x1, Pallas kernels: 58.6 us -> 50 us  [cross_spectra(): pl.pallas_call(functools.partial(window_kernel, devices), out_shape=(jax....]
    pallas_call x1, Pallas kernels: 9.21 us -> 7.98 us  [lag_image(): pl.pallas_call(functools.partial(image_kernel, slots ** (-0.5)), out_shap...]
    another operation x1 -> x0, other arithmetic: 0.81 us -> none
where the time goes in v1:
time: 58.2 us; the launch traced here: 58 us
  Pallas kernels  58 us (100%)
    pallas_call x1, Pallas kernels, cross_spectra(): pl.pallas_call(functools.partial(window_kernel, devices), out_shape=(jax....  50 us
    pallas_call x1, Pallas kernels, lag_image(): pl.pallas_call(functools.partial(image_kernel, slots ** (-0.5)), out_shap...  7.98 us

profile of v1, /device:TPU:0, one launch (start us, length us, event | category | flops | bytes accessed | tf_op | source)
XLA Modules:
  0.0 58.0 jit_solution(11210971083912227449)
XLA Ops:
  0.0 50.0 %shard_map.109 = (bf16[2,16,2,32,256]{4,3,2,1,0:T(8,128)(2,1)S(1)}, bf16[32,256]{1,0:T(8,128)(2,1)S(1)}) custom-call(s32[16]{0:T(128)} %bins.1, f32[2,3]{1,0:T(2,128)} %gaps.1, s32[2]{0:T(128)} %slab_map.1, s32[2]{0:T(128)} %corner.1, bf16[1,768,512]{2,1,0:T(8,128)(2,1)} %slab_in.1, bf16[2,512,256]{2,1,0:T(8,128)(2,1)} %bitcast.2, ...), custom_call_target="tpu_custom_call" | custom-call | flops 51539607552 | bytes 8388608 | tf_op jit(solution)/shard_map/pallas_call | solution.py:512
  50.0 8.0 %shard_map.110 = f32[2,32,256,256]{3,2,1,0:T(8,128)} custom-call(bf16[2,16,2,32,256]{4,3,2,1,0:T(8,128)(2,1)S(1)} %get-tuple-element.7.crosses, bf16[32,256]{1,0:T(8,128)(2,1)S(1)} %get-tuple-element.8.weights), custom_call_target="tpu_custom_call" | custom-call | tf_op jit(solution)/shard_map/pallas_call | solution.py:588

commit v2 on v1

--- a/solution.py
+++ b/solution.py
@@ -20,11 +20,6 @@
 tile = 256
 
 
-def spectral_order(length):
-    half = length // 2
-    return np.concatenate([np.arange(half), [half], np.arange(length - 1, half, -1)])
-
-
 def parts_of(length):
     steps = np.arange(length, dtype=np.int64)
     phases = np.mod(steps[:, None] * steps[None, :], length).astype(np.float32)
@@ -33,18 +28,13 @@
     return np.cos(angles) * scale, np.sin(angles) * scale
 
 
-def transform_block(length):
-    cosine, sine = parts_of(length)
-    return np.block([[cosine, -sine], [sine, cosine]]).astype(jnp.bfloat16)
-
-
-def transform_pair(length):
-    cosine, sine = parts_of(length)
-    order = spectral_order(length)
-    return (
-        np.concatenate([cosine[order], sine[order]], axis=1).astype(jnp.bfloat16),
-        np.concatenate([cosine[:, order], sine[:, order]], axis=1).astype(jnp.bfloat16),
-    )
+def real_transform(length):
+    cosine, sine = (part.astype(jnp.bfloat16) for part in parts_of(length))
+    half = length // 2
+    basis = np.concatenate([cosine[: half + 1], sine[1:half]], axis=0)
+    twice = np.full((length, 1), 2.0, np.float32)
+    twice[0] = twice[half] = 1.0
+    return (basis.astype(np.float32) * twice).astype(jnp.bfloat16), basis.T
 
 
 def sin_cos(angle):
@@ -72,10 +62,10 @@
 
 def window_kernel(
     devices, bins, gaps, slab_map, corner, slab_in, source_in, table_y_in, receiver_in,
-    table_f_in, table_i_in, bracket_in,
+    table_f_in, table_i_in, bracket_in, table_z_in,
     received, weights,
-    slab, source, table_y, receiver, table_f, table_i, bracket,
-    half, spectrum, shifted_a, shifted_b, shifted_c, returned, refocused, fields, cross,
+    slab, source, table_y, receiver, table_f, table_i, bracket, table_z,
+    half, spectrum, phases, shifted, returned, refocused, fields, cross,
     wide, windows, pair, part, parts, total, slow, phase_rows,
     load_sems, pair_sems, scatter_sems, gather_sems, cross_sems,
 ):
@@ -93,7 +83,6 @@
     tiles = rows_x // tile
     group = max(share_rows, chunk)
     groups = tile // group
-    shifted = (shifted_a, shifted_b, shifted_c)
     angular = bins[me].astype(jnp.float32) * (2.0 * math.pi * bin_hertz)
     references = []
     for d in range(depths):
@@ -106,12 +95,12 @@
         pltpu.make_async_copy(far, near, load_sems.at[place])
         for place, (far, near) in enumerate((
             (slab_in, slab), (source_in, source), (table_y_in, table_y), (receiver_in, receiver),
-            (table_f_in, table_f), (bracket_in, bracket), (table_i_in, table_i),
+            (table_f_in, table_f), (bracket_in, bracket), (table_i_in, table_i), (table_z_in, table_z),
         ))
     ]
 
-    def lanes(which):
-        return pl.ds(which * cols_y, cols_y)
+    def lanes(which, side):
+        return pl.ds((2 * which + side) * cols_y, cols_y)
 
     def remote(source_ref, target_ref, sems, place):
         return pltpu.make_async_remote_copy(
@@ -242,12 +231,13 @@
         swap_first(d).start()
 
     columns = lax.broadcasted_iota(jnp.int32, (chunk, cols_y), 1)
-    wave_y = jnp.where(columns < cols_y // 2, columns, cols_y - columns).astype(jnp.float32) * (
-        2.0 * math.pi / (cols_y * cell_width)
-    )
+    wave_y = jnp.where(columns <= cols_y // 2, columns, columns - cols_y // 2).astype(
+        jnp.float32
+    ) * (2.0 * math.pi / (cols_y * cell_width))
     squares_y = wave_y * wave_y
-
-    def phases(d, ref, magnitude):
+    counted = lax.broadcasted_iota(jnp.int32, (chunk, cols_y), 0)
+
+    def phase_chunk(d, ref, start, magnitude):
         wave_x = magnitude.astype(jnp.float32) * (2.0 * math.pi / (rows_x * cell_width))
         reach = angular * references[d][ref]
         radicand = reach * reach - (wave_x * wave_x + squares_y)
@@ -255,36 +245,46 @@
         moving = radicand > 0.0
         fading = jnp.exp(jnp.where(moving, 0.0, -depth))
         sine, cosine = sin_cos(jnp.where(moving, depth, 0.0) - reach * layer_thick)
-        return fading * cosine, fading * sine
-
-    def apply_phase(target, cosine, sine, start):
+        phases[d, ref, 0, pl.ds(start, chunk), :] = fading * cosine
+        phases[d, ref, 1, pl.ds(start, chunk), :] = fading * sine
+
+    def phase_table(d, ref):
+        @pl.loop(0, middle // chunk)
+        def _(number):
+            start = pl.multiple_of(number * chunk, chunk)
+            phase_chunk(d, ref, start, counted + start)
+
+        phase_chunk(d, ref, middle, jnp.where(counted == 0, middle, counted))
+
+    def apply_phase(d, ref, start, place):
         rows = pl.ds(start, chunk)
-        low_rows = pl.ds(rows_x + start, chunk)
+        cosine = phases[d, ref, 0, pl.ds(place, chunk), :]
+        sine = phases[d, ref, 1, pl.ds(place, chunk), :]
         for which in range(2):
             turned = signs[which] * sine
-            real = spectrum[rows, lanes(which)]
-            imag = spectrum[low_rows, lanes(which)]
-            new_real = (cosine * real - turned * imag).astype(jnp.bfloat16)
-            target[rows, lanes(which)] = new_real
-            target[low_rows, lanes(which)] = (-(cosine * imag + turned * real)).astype(jnp.bfloat16)
-            target[pl.ds(2 * rows_x + start, chunk), lanes(which)] = -new_real
-
-    counted = lax.broadcasted_iota(jnp.int32, (chunk, cols_y), 0)
-
-    def shift_chunk(d, ref, target, start):
-        cosine, sine = phases(d, ref, counted + start)
-        apply_phase(target, cosine, sine, start)
-        apply_phase(target, cosine, sine, pl.multiple_of(middle + start, chunk))
-
-    def shift_edge(d, ref, target):
-        cosine, sine = phases(d, ref, jnp.where(counted == 0, middle, counted))
-        apply_phase(target, cosine, sine, middle)
-
-    def multiply(table, values, rows):
-        block = table[rows, :]
-        real = jnp.dot(block, values[: 2 * rows_x, :], preferred_element_type=jnp.float32)
-        imag = jnp.dot(block, values[rows_x:, :], preferred_element_type=jnp.float32)
-        return real, imag
+            real = spectrum[rows, lanes(which, 0)]
+            imag = spectrum[rows, lanes(which, 1)]
+            shifted[ref, rows, lanes(which, 0)] = (cosine * real - turned * imag).astype(
+                jnp.bfloat16
+            )
+            shifted[ref, rows, lanes(which, 1)] = (cosine * imag + turned * real).astype(
+                jnp.bfloat16
+            )
+
+    def shift_chunk(d, ref, start):
+        apply_phase(d, ref, start, start)
+        apply_phase(d, ref, pl.multiple_of(middle + start, chunk), start)
+
+    def shift_edge(d, ref):
+        apply_phase(d, ref, 0, 0)
+        apply_phase(d, ref, middle, middle)
+
+    def shift(d, ref):
+        @pl.loop(1, middle // chunk)
+        def _(number):
+            shift_chunk(d, ref, pl.multiple_of(number * chunk, chunk))
+
+        shift_edge(d, ref)
 
     def slow_rows(d, start):
         if share_rows >= chunk:
@@ -328,15 +328,15 @@
         for which in range(2):
             mixed = []
             for side in range(2):
-                first = refocused[turn, 0, which, local, lanes(side)]
-                second = refocused[turn, 1, which, local, lanes(side)]
-                third = refocused[turn, 2, which, local, lanes(side)]
+                first = refocused[turn, 0, local, lanes(which, side)]
+                second = refocused[turn, 1, local, lanes(which, side)]
+                third = refocused[turn, 2, local, lanes(which, side)]
                 low = jnp.where(lower, first, second)
                 high = jnp.where(lower, second, third)
                 mixed.append((1.0 - weight) * low + weight * high)
             turned = signs[which] * sine
-            real = (cosine * mixed[0] + turned * mixed[1]).astype(jnp.bfloat16)
-            imag = (turned * mixed[0] - cosine * mixed[1]).astype(jnp.bfloat16)
+            real = (cosine * mixed[0] - turned * mixed[1]).astype(jnp.bfloat16)
+            imag = (turned * mixed[0] + cosine * mixed[1]).astype(jnp.bfloat16)
             if d < depths - 1:
                 fields[which, 0, rows, :] = real
                 fields[which, 1, rows, :] = imag
@@ -346,58 +346,31 @@
         store_cross(d, start, 1, sr * ri - si * rr)
 
     def forward_y(which, field):
-        for start in range(0, rows_x, tile):
-            rows = pl.ds(start, tile)
-            both = jnp.concatenate([field[0, rows, :], field[1, rows, :]], axis=1)
-            out = jnp.dot(both, table_y[...], preferred_element_type=jnp.float32)
-            out = out.astype(jnp.bfloat16)
-            half[rows, lanes(which)] = out[:, :cols_y]
-            half[pl.ds(rows_x + start, tile), lanes(which)] = out[:, cols_y:]
-            half[pl.ds(2 * rows_x + start, tile), lanes(which)] = -out[:, :cols_y]
+        for side in range(2):
+            for start in range(0, rows_x, tile):
+                rows = pl.ds(start, tile)
+                half[rows, lanes(which, side)] = jnp.dot(
+                    field[side, rows, :], table_y[...], preferred_element_type=jnp.float32
+                ).astype(jnp.bfloat16)
 
     def forward_x():
         @pl.loop(0, rows_x // tile)
         def _(number):
-            start = pl.multiple_of(number * tile, tile)
-            real, imag = multiply(table_f, half, pl.ds(start, tile))
-            spectrum[pl.ds(start, tile), :] = real
-            spectrum[pl.ds(rows_x + start, tile), :] = imag
-
-    def shift_first(d):
-        @pl.loop(0, middle // chunk)
-        def _(number):
-            shift_chunk(d, 0, shifted[0], pl.multiple_of(number * chunk, chunk))
-
-        shift_edge(d, 0, shifted[0])
-
-    def inverse(d, turn, ref, tile_start):
-        if turn == 0 and ref < 2:
-            part_rows = tile // 2
-
-            @pl.loop(0, 2)
-            def _(side):
-                inner = pl.multiple_of(side * part_rows, part_rows)
-                real, imag = multiply(table_i, shifted[ref], pl.ds(tile_start + inner, part_rows))
-                returned[pl.ds(inner, part_rows), :] = real.astype(jnp.bfloat16)
-                returned[pl.ds(tile + inner, part_rows), :] = imag.astype(jnp.bfloat16)
-                for each in range(middle // chunk // 2):
-                    shift_chunk(
-                        d, ref + 1, shifted[ref + 1],
-                        pl.multiple_of(side * (middle // 2) + each * chunk, chunk),
-                    )
-
-            shift_edge(d, ref + 1, shifted[ref + 1])
-        else:
-            real, imag = multiply(table_i, shifted[ref], pl.ds(tile_start, tile))
-            returned[:tile, :] = real.astype(jnp.bfloat16)
-            returned[tile:, :] = imag.astype(jnp.bfloat16)
+            rows = pl.ds(pl.multiple_of(number * tile, tile), tile)
+            spectrum[rows, :] = jnp.dot(
+                table_f[rows, :], half[...], preferred_element_type=jnp.float32
+            )
+
+    def inverse(turn, ref, tile_start):
+        returned[...] = jnp.dot(
+            table_i[pl.ds(tile_start, tile), :], shifted[ref], preferred_element_type=jnp.float32
+        ).astype(jnp.bfloat16)
         for which in range(2):
-            both = jnp.concatenate(
-                [returned[:tile, lanes(which)], returned[tile:, lanes(which)]], axis=1
-            )
-            refocused[turn, ref, which] = jnp.dot(
-                both, table_y[...], preferred_element_type=jnp.float32
-            )
+            for side in range(2):
+                refocused[turn, ref, :, lanes(which, side)] = jnp.dot(
+                    returned[:, lanes(which, side)], table_z[...],
+                    preferred_element_type=jnp.float32,
+                )
 
     def send_group(d, tile_start, index):
         for each in range(group // share_rows):
@@ -453,24 +426,29 @@
             loads[1].wait()
             loads[2].wait()
             forward_y(0, source)
-            begin_scatter(0)
             loads[3].wait()
             forward_y(1, receiver)
+            begin_scatter(0)
             loads[4].wait()
             forward_x()
-            shift_first(0)
+            for ref in range(3):
+                phase_table(0, ref)
+                shift(0, ref)
             begin_gather(0)
             for later in range(1, depths):
                 begin_scatter(later)
             loads[5].wait()
             loads[6].wait()
+            loads[7].wait()
             for turn in range(tiles):
                 for ref in range(3):
-                    if turn == tiles - 1 and ref == 2:
-                        begin_last(0)
-                        for later in range(1, depths):
-                            begin_gather(later)
-                    inverse(0, turn, ref, tile_starts[turn])
+                    inverse(turn, ref, tile_starts[turn])
+            for later in range(1, depths):
+                for ref in range(3):
+                    phase_table(later, ref)
+            begin_last(0)
+            for later in range(1, depths):
+                begin_gather(later)
             lag_table()
             swap_last(0).wait()
             for turn in range(tiles):
@@ -481,10 +459,11 @@
             forward_y(0, fields.at[0])
             forward_y(1, fields.at[1])
             forward_x()
-            shift_first(d)
+            for ref in range(3):
+                shift(d, ref)
             for turn in range(tiles):
                 for ref in range(3):
-                    inverse(d, turn, ref, tile_starts[turn])
+                    inverse(turn, ref, tile_starts[turn])
                 if turn == 0:
                     swap_last(d).wait()
                 mix_tile(d, turn, tile_starts[turn])
@@ -502,10 +481,10 @@
     slab_count, rows_all, cols_all = slabs.shape
     chips = devices // 2
     share_rows = rows_x // devices
-    table_f, table_i = transform_pair(rows_x)
-    table_y = transform_block(cols_y)
+    table_f, table_i = real_transform(rows_x)
+    table_y, table_z = (table.T for table in real_transform(cols_y))
     vmem = pl.BlockSpec(memory_space=pltpu.VMEM)
-    flops = 16 * rows_x * (2 * rows_x + 2 * cols_y) * 2 * cols_y * depths
+    flops = 8 * rows_x * (rows_x + cols_y) * 4 * cols_y * depths
     dma = pltpu.SemaphoreType.DMA
     held = (depths, chips, share_rows, cols_y)
     field = pltpu.VMEM((2, rows_x, cols_y), jnp.bfloat16)
@@ -516,7 +495,7 @@
             jax.ShapeDtypeStruct((2 * devices, LAGS), jnp.bfloat16),
         ),
         in_specs=[pl.BlockSpec(memory_space=pltpu.SMEM)] * 4
-        + [pl.BlockSpec(memory_space=pltpu.HBM)] * 7,
+        + [pl.BlockSpec(memory_space=pltpu.HBM)] * 8,
         out_specs=(vmem, vmem),
         scratch_shapes=[
             pltpu.VMEM(slabs.shape, jnp.bfloat16),
@@ -526,13 +505,13 @@
             pltpu.VMEM(table_f.shape, jnp.bfloat16),
             pltpu.VMEM(table_i.shape, jnp.bfloat16),
             pltpu.VMEM(bracket.shape, jnp.int32),
-            pltpu.VMEM((3 * rows_x, 2 * cols_y), jnp.bfloat16),
-            pltpu.VMEM((2 * rows_x, 2 * cols_y), jnp.float32),
-            pltpu.VMEM((3 * rows_x, 2 * cols_y), jnp.bfloat16),
-            pltpu.VMEM((3 * rows_x, 2 * cols_y), jnp.bfloat16),
-            pltpu.VMEM((3 * rows_x, 2 * cols_y), jnp.bfloat16),
-            pltpu.VMEM((2 * tile, 2 * cols_y), jnp.bfloat16),
-            pltpu.VMEM((rows_x // tile, 3, 2, tile, 2 * cols_y), jnp.float32),
+            pltpu.VMEM(table_z.shape, jnp.bfloat16),
+            pltpu.VMEM((rows_x, 4 * cols_y), jnp.bfloat16),
+            pltpu.VMEM((rows_x, 4 * cols_y), jnp.float32),
+            pltpu.VMEM((depths, 3, 2, rows_x // 2 + chunk, cols_y), jnp.float32),
+            pltpu.VMEM((3, rows_x, 4 * cols_y), jnp.bfloat16),
+            pltpu.VMEM((tile, 4 * cols_y), jnp.bfloat16),
+            pltpu.VMEM((rows_x // tile, 3, tile, 4 * cols_y), jnp.float32),
             pltpu.VMEM((2, 2, rows_x, cols_y), jnp.bfloat16),
             pltpu.VMEM((depths, devices, 2, share_rows, cols_y), jnp.bfloat16),
             pltpu.VMEM((rows_all, cols_y), jnp.bfloat16),
@@ -543,14 +522,14 @@
             pltpu.VMEM((depths, share_rows, cols_y), jnp.bfloat16),
             pltpu.VMEM((depths, 2, chips, share_rows, cols_y), jnp.bfloat16),
             pltpu.VMEM((2 * devices, LAGS), jnp.float32),
-            dma((7,)),
+            dma((8,)),
             dma((depths, 4)),
             dma((depths, 2, chips)),
             dma((depths, 2, chips)),
             dma((depths, 2, devices)),
         ],
         cost_estimate=pl.CostEstimate(
-            flops=4 * flops, bytes_accessed=8 * 1024 * 1024, transcendentals=0
+            flops=flops, bytes_accessed=8 * 1024 * 1024, transcendentals=0
         ),
         compiler_params=pltpu.CompilerParams(
             collective_id=0, has_side_effects=True, vmem_limit_bytes=44 * 1024 * 1024
@@ -560,7 +539,7 @@
             pltpu.with_memory_space_constraint(value, pltpu.HBM)
             for value in (
                 bins, gaps, slab_map, corner, slabs, source, jnp.asarray(table_y), receiver,
-                jnp.asarray(table_f), jnp.asarray(table_i), bracket,
+                jnp.asarray(table_f), jnp.asarray(table_i), bracket, jnp.asarray(table_z),
             )
         ]
     )

time: 58.2 us -> 58.1 us (level)
  no operation moved by 1% of the time
where the time goes in v2:
time: 58.1 us; the launch traced here: 57.9 us
  Pallas kernels  57.9 us (100%)
    pallas_call x1, Pallas kernels, cross_spectra(): pl.pallas_call(functools.partial(window_kernel, devices), out_shape=(jax....  50 us
    pallas_call x1, Pallas kernels, lag_image(): pl.pallas_call(functools.partial(image_kernel, slots ** (-0.5)), out_shap...  7.95 us

profile of v2, /device:TPU:0, one launch (start us, length us, event | category | flops | bytes accessed | tf_op | source)
XLA Modules:
  0.0 57.9 jit_solution(6308779913643176604)
XLA Ops:
  0.0 50.0 %shard_map.118 = (bf16[2,16,2,32,256]{4,3,2,1,0:T(8,128)(2,1)S(1)}, bf16[32,256]{1,0:T(8,128)(2,1)S(1)}) custom-call(s32[16]{0:T(128)} %bins.1, f32[2,3]{1,0:T(2,128)} %gaps.1, s32[2]{0:T(128)} %slab_map.1, s32[2]{0:T(128)} %corner.1, bf16[1,768,512]{2,1,0:T(8,128)(2,1)} %slab_in.1, bf16[2,512,256]{2,1,0:T(8,128)(2,1)} %bitcast.2, ...), custom_call_target="tpu_custom_call" | custom-call | flops 6442450944 | bytes 8388608 | tf_op jit(solution)/shard_map/pallas_call | solution.py:491
  50.0 8.0 %shard_map.119 = f32[2,32,256,256]{3,2,1,0:T(8,128)} custom-call(bf16[2,16,2,32,256]{4,3,2,1,0:T(8,128)(2,1)S(1)} %get-tuple-element.7.crosses, bf16[32,256]{1,0:T(8,128)(2,1)S(1)} %get-tuple-element.8.weights), custom_call_target="tpu_custom_call" | custom-call | tf_op jit(solution)/shard_map/pallas_call | solution.py:567

commit v3 on v2

--- a/solution.py
+++ b/solution.py
@@ -67,7 +67,7 @@
     slab, source, table_y, receiver, table_f, table_i, bracket, table_z,
     half, spectrum, phases, shifted, returned, refocused, fields, cross,
     wide, windows, pair, part, parts, total, slow, phase_rows,
-    load_sems, pair_sems, scatter_sems, gather_sems, cross_sems,
+    load_sems, pair_sems, scatter_sems, gather_sems, trade_sems, cross_sems,
 ):
     depths, rows_x, cols_y = bracket.shape
     slab_count, rows_all, cols_all = slab.shape
@@ -142,6 +142,70 @@
             (cross_sems.at[d, 0, hop], cross_sems.at[d, 1, hop]), to,
         )
 
+    levels = chips.bit_length() - 1
+
+    def bit_of(level):
+        return lax.rem(chip // 2**level, 2)
+
+    def lowest(level):
+        return sum((bit_of(below) * (chips >> (below + 1)) for below in range(level)), 0 * chip)
+
+    def trade(d, step, source_ref, target_ref):
+        level = step if step < levels else 2 * levels - 2 - step
+        place = chip + (1 - 2 * bit_of(level)) * 2**level
+        return remote(
+            source_ref, target_ref, (trade_sems.at[d, 0, step], trade_sems.at[d, 1, step]),
+            place * 2 + core,
+        )
+
+    def halve(d, level):
+        size = chips >> (level + 1)
+        sent = lowest(level) + (1 - bit_of(level)) * size
+        return trade(
+            d, level, part.at[d, pl.ds(sent, size)],
+            parts.at[d, pl.ds(chips - (chips >> level), size)],
+        )
+
+    def add_half(d, level):
+        size = chips >> (level + 1)
+        kept = pl.ds(lowest(level + 1), size)
+        part[d, kept] = part[d, kept] + parts[d, pl.ds(chips - (chips >> level), size)]
+
+    def exchange(d):
+        kept = pl.ds(lowest(levels - 1), 2)
+        return trade(d, levels - 1, part.at[d, kept], parts.at[d, pl.ds(chips - 2, 2)])
+
+    def double(d, level):
+        ready = pl.ds(lowest(level + 1), chips >> (level + 1))
+        return trade(
+            d, 2 * levels - 2 - level, slow.at[d, core, ready], slow.at[d, core, ready]
+        )
+
+    def relay(d):
+        swap_first(d).wait()
+        part[d] = windows[d, core] + pair[d]
+        for level in range(levels - 1):
+            halve(d, level).start()
+            yield
+            halve(d, level).wait()
+            add_half(d, level)
+        exchange(d).start()
+        yield
+        exchange(d).wait()
+        kept = pl.ds(lowest(levels - 1), 2)
+        slow[d, core, kept] = part[d, kept] + parts[d, pl.ds(chips - 2, 2)]
+        for level in reversed(range(levels - 1)):
+            double(d, level).start()
+            yield
+            double(d, level).wait()
+        swap_last(d).start()
+
+    relays = [relay(d) for d in range(1, depths)]
+
+    def advance():
+        for each in relays:
+            next(each, None)
+
     def begin_scatter(d):
         swap_first(d).wait()
         part[d] = windows[d, core] + pair[d]
@@ -181,8 +245,7 @@
             device_id_type=pl.DeviceIdType.MESH,
         )
 
-    for load in loads:
-        load.start()
+    loads[0].start()
 
     def one_hot(sizes, offset):
         ahead = lax.broadcasted_iota(jnp.int32, sizes, 0) - lax.broadcasted_iota(
@@ -203,22 +266,23 @@
         for d in steps:
             apart = jnp.abs(lax.div(slab_map[d], slab_count) - me)
             kept.append((1 - jnp.minimum(apart, 1)).astype(jnp.float32))
-        size = max(share_rows, chunk)
-
-        @pl.loop(0, rows_x // size)
-        def _(number):
-            start = number * size
-            pick = one_hot((size, rows_all), -(corner[0] + start))
-            values = jnp.dot(pick, wide[...], preferred_element_type=jnp.float32)
+        reach = tile + rows_all - rows_x
+        pick = one_hot((tile, reach), -corner[0])
+        for start in range(0, rows_x, tile):
+            values = jnp.dot(
+                pick, wide[pl.ds(start, reach), :], preferred_element_type=jnp.float32
+            )
             for d, keep in zip(steps, kept):
                 held = (values * keep).astype(jnp.bfloat16)
-                for piece in range(size // share_rows):
+                for piece in range(tile // share_rows):
                     block = start // share_rows + piece
-                    windows[d, block // chips, lax.rem(block, chips)] = held[
+                    windows[d, block // chips, block % chips] = held[
                         piece * share_rows : (piece + 1) * share_rows
                     ]
 
     loads[0].wait()
+    for load in loads[1:]:
+        load.start()
     if slab_count == 1:
         cut_slab(0)
         put_windows(range(depths))
@@ -418,47 +482,55 @@
         odd = lax.broadcasted_iota(jnp.int32, counts.shape, 0) % 2 == 1
         weights[...] = jnp.where(odd, -sine, cosine).astype(jnp.bfloat16)
 
-    tile_starts = [
-        pl.multiple_of(lax.rem(own_tile + 1 + turn, tiles) * tile, tile) for turn in range(tiles)
-    ]
+    first_tiles = (core * (tiles // 2),) + (own_tile + 1,) * (depths - 1)
     for d in range(depths):
+        tile_starts = [
+            pl.multiple_of(lax.rem(first_tiles[d] + turn, tiles) * tile, tile)
+            for turn in range(tiles)
+        ]
         if d == 0:
             loads[1].wait()
             loads[2].wait()
             forward_y(0, source)
+            begin_scatter(0)
+            advance()
             loads[3].wait()
             forward_y(1, receiver)
-            begin_scatter(0)
             loads[4].wait()
             forward_x()
             for ref in range(3):
                 phase_table(0, ref)
+            advance()
+            for ref in range(3):
                 shift(0, ref)
             begin_gather(0)
-            for later in range(1, depths):
-                begin_scatter(later)
             loads[5].wait()
             loads[6].wait()
             loads[7].wait()
             for turn in range(tiles):
                 for ref in range(3):
                     inverse(turn, ref, tile_starts[turn])
+                if turn == 0:
+                    advance()
             for later in range(1, depths):
                 for ref in range(3):
                     phase_table(later, ref)
+            advance()
+            lag_table()
             begin_last(0)
-            for later in range(1, depths):
-                begin_gather(later)
-            lag_table()
+            for turn in range(tiles // 2):
+                mix_tile(0, turn, tile_starts[turn])
             swap_last(0).wait()
-            for turn in range(tiles):
+            advance()
+            for turn in range(tiles // 2, tiles):
                 mix_tile(0, turn, tile_starts[turn])
-            for later in range(1, depths):
-                begin_last(later)
         else:
             forward_y(0, fields.at[0])
             forward_y(1, fields.at[1])
             forward_x()
+            if d == 1:
+                for _ in range(2 * levels):
+                    advance()
             for ref in range(3):
                 shift(d, ref)
             for turn in range(tiles):
@@ -526,6 +598,7 @@
             dma((depths, 4)),
             dma((depths, 2, chips)),
             dma((depths, 2, chips)),
+            dma((depths, 2, 2 * chips.bit_length() - 3)),
             dma((depths, 2, devices)),
         ],
         cost_estimate=pl.CostEstimate(
@@ -562,7 +635,7 @@
 def lag_image(crosses, weights):
     depths, slots, _, rows, cols_y = crosses.shape
     lag_count = weights.shape[1]
-    step = min(8, rows)
+    step = min(16, rows)
     whole = pl.BlockSpec(memory_space=pltpu.VMEM)
     return pl.pallas_call(
         functools.partial(image_kernel, slots ** (-0.5)),

time: 58.1 us -> 53.2 us (0.916)
  Pallas kernels: 57.9 us -> 53.1 us
    pallas_call x1, Pallas kernels: 50 us -> 46.1 us  [cross_spectra(): pl.pallas_call(functools.partial(window_kernel, devices), out_shape=(jax....]
    pallas_call x1, Pallas kernels: 7.95 us -> 6.97 us  [lag_image(): pl.pallas_call(functools.partial(image_kernel, slots ** (-0.5)), out_shap...]
where the time goes in v3:
time: 53.2 us; the launch traced here: 53.1 us
  Pallas kernels  53.1 us (100%)
    pallas_call x1, Pallas kernels, cross_spectra(): pl.pallas_call(functools.partial(window_kernel, devices), out_shape=(jax....  46.1 us
    pallas_call x1, Pallas kernels, lag_image(): pl.pallas_call(functools.partial(image_kernel, slots ** (-0.5)), out_shap...  6.97 us

profile of v3, /device:TPU:0, one launch (start us, length us, event | category | flops | bytes accessed | tf_op | source)
XLA Modules:
  0.0 53.1 jit_solution(11637205402804431231)
XLA Ops:
  0.0 46.1 %shard_map.118 = (bf16[2,16,2,32,256]{4,3,2,1,0:T(8,128)(2,1)S(1)}, bf16[32,256]{1,0:T(8,128)(2,1)S(1)}) custom-call(s32[16]{0:T(128)} %bins.1, f32[2,3]{1,0:T(2,128)} %gaps.1, s32[2]{0:T(128)} %slab_map.1, s32[2]{0:T(128)} %corner.1, bf16[1,768,512]{2,1,0:T(8,128)(2,1)} %slab_in.1, bf16[2,512,256]{2,1,0:T(8,128)(2,1)} %bitcast.2, ...), custom_call_target="tpu_custom_call" | custom-call | flops 6442450944 | bytes 8388608 | tf_op jit(solution)/shard_map/pallas_call | solution.py:563
  46.1 7.0 %shard_map.119 = f32[2,32,256,256]{3,2,1,0:T(8,128)} custom-call(bf16[2,16,2,32,256]{4,3,2,1,0:T(8,128)(2,1)S(1)} %get-tuple-element.7.crosses, bf16[32,256]{1,0:T(8,128)(2,1)S(1)} %get-tuple-element.8.weights), custom_call_target="tpu_custom_call" | custom-call | tf_op jit(solution)/shard_map/pallas_call | solution.py:640

commit v4 on v2

--- a/solution.py
+++ b/solution.py
@@ -181,8 +181,7 @@
             device_id_type=pl.DeviceIdType.MESH,
         )
 
-    for load in loads:
-        load.start()
+    loads[0].start()
 
     def one_hot(sizes, offset):
         ahead = lax.broadcasted_iota(jnp.int32, sizes, 0) - lax.broadcasted_iota(
@@ -203,22 +202,23 @@
         for d in steps:
             apart = jnp.abs(lax.div(slab_map[d], slab_count) - me)
             kept.append((1 - jnp.minimum(apart, 1)).astype(jnp.float32))
-        size = max(share_rows, chunk)
-
-        @pl.loop(0, rows_x // size)
-        def _(number):
-            start = number * size
-            pick = one_hot((size, rows_all), -(corner[0] + start))
-            values = jnp.dot(pick, wide[...], preferred_element_type=jnp.float32)
+        reach = tile + rows_all - rows_x
+        pick = one_hot((tile, reach), -corner[0])
+        for start in range(0, rows_x, tile):
+            values = jnp.dot(
+                pick, wide[pl.ds(start, reach), :], preferred_element_type=jnp.float32
+            )
             for d, keep in zip(steps, kept):
                 held = (values * keep).astype(jnp.bfloat16)
-                for piece in range(size // share_rows):
+                for piece in range(tile // share_rows):
                     block = start // share_rows + piece
-                    windows[d, block // chips, lax.rem(block, chips)] = held[
+                    windows[d, block // chips, block % chips] = held[
                         piece * share_rows : (piece + 1) * share_rows
                     ]
 
     loads[0].wait()
+    for load in loads[1:]:
+        load.start()
     if slab_count == 1:
         cut_slab(0)
         put_windows(range(depths))
@@ -418,25 +418,27 @@
         odd = lax.broadcasted_iota(jnp.int32, counts.shape, 0) % 2 == 1
         weights[...] = jnp.where(odd, -sine, cosine).astype(jnp.bfloat16)
 
-    tile_starts = [
-        pl.multiple_of(lax.rem(own_tile + 1 + turn, tiles) * tile, tile) for turn in range(tiles)
-    ]
+    first_tiles = (core * (tiles // 2),) + (own_tile + 1,) * (depths - 1)
     for d in range(depths):
+        tile_starts = [
+            pl.multiple_of(lax.rem(first_tiles[d] + turn, tiles) * tile, tile)
+            for turn in range(tiles)
+        ]
         if d == 0:
             loads[1].wait()
             loads[2].wait()
             forward_y(0, source)
+            begin_scatter(0)
             loads[3].wait()
             forward_y(1, receiver)
-            begin_scatter(0)
             loads[4].wait()
             forward_x()
+            for later in range(1, depths):
+                begin_scatter(later)
             for ref in range(3):
                 phase_table(0, ref)
                 shift(0, ref)
             begin_gather(0)
-            for later in range(1, depths):
-                begin_scatter(later)
             loads[5].wait()
             loads[6].wait()
             loads[7].wait()
@@ -444,14 +446,16 @@
                 for ref in range(3):
                     inverse(turn, ref, tile_starts[turn])
             for later in range(1, depths):
+                begin_gather(later)
+            for later in range(1, depths):
                 for ref in range(3):
                     phase_table(later, ref)
+            lag_table()
             begin_last(0)
-            for later in range(1, depths):
-                begin_gather(later)
-            lag_table()
+            for turn in range(tiles // 2):
+                mix_tile(0, turn, tile_starts[turn])
             swap_last(0).wait()
-            for turn in range(tiles):
+            for turn in range(tiles // 2, tiles):
                 mix_tile(0, turn, tile_starts[turn])
             for later in range(1, depths):
                 begin_last(later)
@@ -562,7 +566,7 @@
 def lag_image(crosses, weights):
     depths, slots, _, rows, cols_y = crosses.shape
     lag_count = weights.shape[1]
-    step = min(8, rows)
+    step = min(16, rows)
     whole = pl.BlockSpec(memory_space=pltpu.VMEM)
     return pl.pallas_call(
         functools.partial(image_kernel, slots ** (-0.5)),

time: 58.1 us -> 51.8 us (0.89)
  Pallas kernels: 57.9 us -> 51.7 us
    pallas_call x1, Pallas kernels: 50 us -> 44.7 us  [cross_spectra(): pl.pallas_call(functools.partial(window_kernel, devices), out_shape=(jax....]
    pallas_call x1, Pallas kernels: 7.95 us -> 6.97 us  [lag_image(): pl.pallas_call(functools.partial(image_kernel, slots ** (-0.5)), out_shap...]
where the time goes in v4:
time: 51.8 us; the launch traced here: 51.7 us
  Pallas kernels  51.7 us (100%)
    pallas_call x1, Pallas kernels, cross_spectra(): pl.pallas_call(functools.partial(window_kernel, devices), out_shape=(jax....  44.7 us
    pallas_call x1, Pallas kernels, lag_image(): pl.pallas_call(functools.partial(image_kernel, slots ** (-0.5)), out_shap...  6.97 us

profile of v4, /device:TPU:0, one launch (start us, length us, event | category | flops | bytes accessed | tf_op | source)
XLA Modules:
  0.0 51.7 jit_solution(9797572424711798096)
XLA Ops:
  0.0 44.7 %shard_map.118 = (bf16[2,16,2,32,256]{4,3,2,1,0:T(8,128)(2,1)S(1)}, bf16[32,256]{1,0:T(8,128)(2,1)S(1)}) custom-call(s32[16]{0:T(128)} %bins.1, f32[2,3]{1,0:T(2,128)} %gaps.1, s32[2]{0:T(128)} %slab_map.1, s32[2]{0:T(128)} %corner.1, bf16[1,768,512]{2,1,0:T(8,128)(2,1)} %slab_in.1, bf16[2,512,256]{2,1,0:T(8,128)(2,1)} %bitcast.2, ...), custom_call_target="tpu_custom_call" | custom-call | flops 6442450944 | bytes 8388608 | tf_op jit(solution)/shard_map/pallas_call | solution.py:495
  44.7 7.0 %shard_map.119 = f32[2,32,256,256]{3,2,1,0:T(8,128)} custom-call(bf16[2,16,2,32,256]{4,3,2,1,0:T(8,128)(2,1)S(1)} %get-tuple-element.7.crosses, bf16[32,256]{1,0:T(8,128)(2,1)S(1)} %get-tuple-element.8.weights), custom_call_target="tpu_custom_call" | custom-call | tf_op jit(solution)/shard_map/pallas_call | solution.py:571

commit v5 on v4

--- a/solution.py
+++ b/solution.py
@@ -18,6 +18,7 @@
 slow_base = 0.3
 chunk = 16
 tile = 256
+strip = 64
 
 
 def parts_of(length):
@@ -37,27 +38,21 @@
     return (basis.astype(np.float32) * twice).astype(jnp.bfloat16), basis.T
 
 
-def sin_cos(angle):
-    turns = jnp.floor(angle * (2.0 / math.pi) + 0.5)
-    rest = angle - turns * 1.5707855224609375
-    rest = rest - turns * 1.0804334124e-05
-    quarter = turns.astype(jnp.int32)
-    square = rest * rest
-    sine = rest + rest * square * (
-        -1.6666654611e-1 + square * (8.3321608736e-3 + square * -1.9515295891e-4)
+def sin_cos(half_angle):
+    square = half_angle * half_angle
+    sine = half_angle + half_angle * square * (
+        -1.6666656999673e-1
+        + square * (8.3330149027548e-3 + square * (-1.9806441580e-4 + square * 2.5996687760e-6))
     )
-    cosine = (
-        1.0
-        - 0.5 * square
-        + square * square
-        * (4.166664568298827e-2 + square * (-1.388731625493765e-3 + square * 2.443315711809948e-5))
+    cosine = 1.0 + square * (
+        -4.9999999543840e-1
+        + square * (
+            4.1666640465459e-2
+            + square * (-1.3888399836750e-3 + square * (2.4761687147e-5 + square * -2.6073429763e-7))
+        )
     )
-    odd = (quarter & 1) == 1
-    sine_out = jnp.where(odd, cosine, sine)
-    cosine_out = jnp.where(odd, sine, cosine)
-    sine_out = jnp.where((quarter & 2) == 2, -sine_out, sine_out)
-    cosine_out = jnp.where(((quarter + 1) & 2) == 2, -cosine_out, cosine_out)
-    return sine_out, cosine_out
+    twice = sine + sine
+    return -(twice * cosine), twice * sine - 1.0
 
 
 def window_kernel(
@@ -65,9 +60,9 @@
     table_f_in, table_i_in, bracket_in, table_z_in,
     received, weights,
     slab, source, table_y, receiver, table_f, table_i, bracket, table_z,
-    half, spectrum, phases, shifted, returned, refocused, fields, cross,
-    wide, windows, pair, part, parts, total, slow, phase_rows,
-    load_sems, pair_sems, scatter_sems, gather_sems, cross_sems,
+    half, spectrum, squares, edge, phases, shifted, returned, refocused, fields, cross,
+    wide, windows, pair, part, parts, traded, total, slow, phase_rows,
+    load_sems, pair_sems, scatter_sems, gather_sems, piece_sems, cross_sems,
 ):
     depths, rows_x, cols_y = bracket.shape
     slab_count, rows_all, cols_all = slab.shape
@@ -108,8 +103,15 @@
             device_id=(grp, place), device_id_type=pl.DeviceIdType.MESH,
         )
 
-    def hop_to(hop):
-        return lax.rem(chip + hop, chips)
+    levels = chips.bit_length() - 1
+    pieced = share_rows >= chunk
+
+    def mate(mask):
+        place = 0 * chip
+        for level in range(levels):
+            flipped = lax.rem(chip // 2**level + mask // 2**level, 2)
+            place = place + flipped * 2**level
+        return place
 
     def swap_first(d):
         return remote(
@@ -117,16 +119,22 @@
             chip * 2 + other,
         )
 
-    def scatter(d, hop):
-        return remote(
-            part.at[d, hop_to(hop)], parts.at[d, hop],
-            (scatter_sems.at[d, 0, hop], scatter_sems.at[d, 1, hop]), hop_to(hop) * 2 + core,
-        )
-
-    def gather(d, hop):
+    def scatter(d, mask):
+        return remote(
+            part.at[d, mate(mask)], parts.at[d, mask],
+            (scatter_sems.at[d, 0, mask], scatter_sems.at[d, 1, mask]), mate(mask) * 2 + core,
+        )
+
+    def gather(d, mask):
         return remote(
             total.at[d], slow.at[d, core, chip],
-            (gather_sems.at[d, 0, hop], gather_sems.at[d, 1, hop]), hop_to(hop) * 2 + core,
+            (gather_sems.at[d, 0, mask], gather_sems.at[d, 1, mask]), mate(mask) * 2 + core,
+        )
+
+    def swap_piece(d, mask):
+        piece = slow.at[d, core, mate(mask)]
+        return remote(
+            piece, piece, (piece_sems.at[0, mask], piece_sems.at[1, mask]), chip * 2 + other
         )
 
     def swap_last(d):
@@ -141,14 +149,77 @@
             cross.at[d, to], received.at[d, me],
             (cross_sems.at[d, 0, hop], cross_sems.at[d, 1, hop]), to,
         )
+
+    sides = chips // 2
+    low = lax.rem(chip, sides)
+    pairs = pl.ds(2 * low, 2)
+    near_start = chip - low
+
+    def near_mate(mask):
+        return lax.rem(mate(mask), sides)
+
+    def near_scatter(d, mask):
+        return remote(
+            part.at[d, pl.ds(2 * near_mate(mask), 2)], parts.at[d, pl.ds(2 * mask, 2)],
+            (scatter_sems.at[d, 0, mask], scatter_sems.at[d, 1, mask]),
+            (near_start + near_mate(mask)) * 2 + core,
+        )
+
+    def trade(d):
+        return remote(
+            parts.at[d, pl.ds(0, 2)], traded.at[d],
+            (scatter_sems.at[d, 0, 0], scatter_sems.at[d, 1, 0]),
+            (sides - near_start + low) * 2 + core,
+        )
+
+    def near_gather(d, mask):
+        return remote(
+            slow.at[d, core, pairs], slow.at[d, core, pairs],
+            (gather_sems.at[d, 0, mask], gather_sems.at[d, 1, mask]),
+            (near_start + near_mate(mask)) * 2 + core,
+        )
+
+    def begin_near_scatter(d):
+        swap_first(d).wait()
+        part[d] = windows[d, core] + pair[d]
+
+        @pl.loop(1, sides)
+        def _(step):
+            near_scatter(d, sides - step).start()
+
+    def begin_trade(d):
+        @pl.loop(1, sides)
+        def _(mask):
+            near_scatter(d, mask).wait()
+
+        summed = part[d, pairs]
+        for mask in range(1, sides):
+            summed = summed + parts[d, pl.ds(2 * mask, 2)]
+        parts[d, pl.ds(0, 2)] = summed
+        trade(d).start()
+
+    def begin_near_gather(d):
+        trade(d).wait()
+        slow[d, core, pairs] = parts[d, pl.ds(0, 2)] + traded[d]
+
+        @pl.loop(1, sides)
+        def _(step):
+            near_gather(d, sides - step).start()
+
+    def begin_near_last(d):
+        @pl.loop(1, sides)
+        def _(mask):
+            near_gather(d, mask).wait()
+
+        swap_last(d).start()
 
     def begin_scatter(d):
         swap_first(d).wait()
         part[d] = windows[d, core] + pair[d]
 
         @pl.loop(1, chips)
-        def _(hop):
-            scatter(d, hop).start()
+        def _(step):
+            scatter(d, chips - step).start()
 
     def begin_gather(d):
         @pl.loop(1, chips)
@@ -162,8 +233,8 @@
         slow[d, core, chip] = summed
 
         @pl.loop(1, chips)
-        def _(hop):
-            gather(d, hop).start()
+        def _(step):
+            gather(d, chips - step).start()
 
     def begin_last(d):
         @pl.loop(1, chips)
@@ -230,31 +301,55 @@
     for d in range(depths):
         swap_first(d).start()
 
-    columns = lax.broadcasted_iota(jnp.int32, (chunk, cols_y), 1)
-    wave_y = jnp.where(columns <= cols_y // 2, columns, columns - cols_y // 2).astype(
-        jnp.float32
-    ) * (2.0 * math.pi / (cols_y * cell_width))
-    squares_y = wave_y * wave_y
-    counted = lax.broadcasted_iota(jnp.int32, (chunk, cols_y), 0)
-
-    def phase_chunk(d, ref, start, magnitude):
-        wave_x = magnitude.astype(jnp.float32) * (2.0 * math.pi / (rows_x * cell_width))
-        reach = angular * references[d][ref]
-        radicand = reach * reach - (wave_x * wave_x + squares_y)
-        depth = jnp.sqrt(jnp.abs(radicand)) * layer_thick
+    half_y = cols_y // 2
+    unit = 0.5 * layer_thick
+    step_x = unit * 2.0 * math.pi / (rows_x * cell_width)
+    step_y = unit * 2.0 * math.pi / (cols_y * cell_width)
+    strips = middle // strip + 1
+    counted = lax.broadcasted_iota(jnp.int32, (strip, half_y), 0)
+    columns = lax.broadcasted_iota(jnp.int32, (strip, half_y), 1)
+
+    def strip_rows(number):
+        return pl.ds(pl.multiple_of(number * strip, strip), strip)
+
+    def reach_of(d, ref):
+        return angular * references[d][ref] * unit
+
+    def turn_of(reach, square):
+        radicand = reach * reach - square
+        size = jnp.abs(radicand)
+        depth = size * lax.rsqrt(jnp.maximum(size, 1e-30))
         moving = radicand > 0.0
-        fading = jnp.exp(jnp.where(moving, 0.0, -depth))
-        sine, cosine = sin_cos(jnp.where(moving, depth, 0.0) - reach * layer_thick)
-        phases[d, ref, 0, pl.ds(start, chunk), :] = fading * cosine
-        phases[d, ref, 1, pl.ds(start, chunk), :] = fading * sine
+        fading = jnp.exp(jnp.where(moving, 0.0, -2.0 * depth))
+        sine, cosine = sin_cos(jnp.where(moving, depth, 0.0) + (0.5 * math.pi - reach))
+        return fading * cosine, fading * sine
+
+    def fill_tables():
+        reach = jnp.zeros((strip, half_y), jnp.float32)
+        for d in range(depths):
+            for ref in range(3):
+                reach = jnp.where(columns == 3 * d + ref, reach_of(d, ref), reach)
+
+        @pl.loop(0, strips)
+        def _(number):
+            rows = strip_rows(number)
+            index = counted + number * strip
+            magnitude = jnp.where(index <= middle, index, index - middle)
+            wave_x = magnitude.astype(jnp.float32) * step_x
+            wave_y = columns.astype(jnp.float32) * step_y
+            squares[rows, :] = wave_x * wave_x + wave_y * wave_y
+            real, imag = turn_of(reach, wave_x * wave_x + (half_y * step_y) ** 2)
+            edge[0, rows, :] = real
+            edge[1, rows, :] = imag
 
     def phase_table(d, ref):
-        @pl.loop(0, middle // chunk)
+        @pl.loop(0, strips)
         def _(number):
-            start = pl.multiple_of(number * chunk, chunk)
-            phase_chunk(d, ref, start, counted + start)
-
-        phase_chunk(d, ref, middle, jnp.where(counted == 0, middle, counted))
+            rows = strip_rows(number)
+            for part, values in enumerate(turn_of(reach_of(d, ref), squares[rows, :])):
+                phases[d, ref, part, rows, :half_y] = values
+                last = pltpu.roll(edge[part, rows, :], (half_y - 3 * d - ref) % half_y, 1)
+                phases[d, ref, part, rows, half_y:] = jnp.where(columns == 0, last, values)
 
     def apply_phase(d, ref, start, place):
         rows = pl.ds(start, chunk)
@@ -319,11 +414,12 @@
         slowness = slow_rows(d, start)
         lower = bracket[d, rows, :] == 0
         slow_low = jnp.where(lower, references[d][0], references[d][1])
-        slow_gap = jnp.where(
-            lower, references[d][1] - references[d][0], references[d][2] - references[d][1]
-        )
-        weight = jnp.clip((slowness - slow_low) / slow_gap, 0.0, 1.0)
-        sine, cosine = sin_cos((angular * layer_thick) * slowness)
+        slow_scale = jnp.where(
+            lower, 1.0 / (references[d][1] - references[d][0]),
+            1.0 / (references[d][2] - references[d][1]),
+        )
+        weight = jnp.clip((slowness - slow_low) * slow_scale, 0.0, 1.0)
+        sine, cosine = sin_cos((angular * unit) * slowness - 0.5 * math.pi)
         rounded = []
         for which in range(2):
             mixed = []
@@ -414,9 +510,41 @@
 
         counts = phase_rows[...]
         wraps = jnp.floor((counts + 0.5) * (1.0 / period_bins))
-        sine, cosine = sin_cos((counts - wraps * period_bins) * (2.0 * math.pi / period_bins))
+        sine, cosine = sin_cos(
+            (counts - wraps * period_bins) * (math.pi / period_bins) - 0.5 * math.pi
+        )
         odd = lax.broadcasted_iota(jnp.int32, counts.shape, 0) % 2 == 1
         weights[...] = jnp.where(odd, -sine, cosine).astype(jnp.bfloat16)
+
+    def mix_piece(d, half, mask):
+        block = mate(mask)
+        turn = (block * share_rows) // tile
+        turn = turn + jnp.where(half == core, 0, tiles // 2)
+        inside = lax.rem(block * share_rows, tile)
+        to = half * chips + block
+        for each in range(share_rows // chunk):
+            mix(
+                d, turn, pl.multiple_of(inside + each * chunk, chunk),
+                pl.multiple_of(to * share_rows + each * chunk, chunk),
+            )
+        hop = lax.rem(to - me + devices, devices)
+
+        @pl.when(hop != 0)
+        def _():
+            send_cross(d, hop).start()
+
+    def mix_pieces(d, first, end):
+        @pl.loop(first, end)
+        def _(mask):
+            gather(d, mask).wait()
+            swap_piece(d, mask).start()
+            mix_piece(d, core, mask)
+            swap_piece(d, mask - 1).wait()
+            mix_piece(d, other, mask - 1)
+
+    def mix_last_piece(d):
+        swap_piece(d, chips - 1).wait()
+        mix_piece(d, other, chips - 1)
 
     first_tiles = (core * (tiles // 2),) + (own_tile + 1,) * (depths - 1)
     for d in range(depths):
@@ -425,6 +553,7 @@
             for turn in range(tiles)
         ]
         if d == 0:
+            fill_tables()
             loads[1].wait()
             loads[2].wait()
             forward_y(0, source)
@@ -434,35 +563,47 @@
             loads[4].wait()
             forward_x()
             for later in range(1, depths):
-                begin_scatter(later)
+                begin_near_scatter(later)
             for ref in range(3):
                 phase_table(0, ref)
                 shift(0, ref)
+            loads[6].wait()
+            loads[7].wait()
+            for turn in range(tiles // 2):
+                for ref in range(3):
+                    inverse(turn, ref, tile_starts[turn])
             begin_gather(0)
             loads[5].wait()
-            loads[6].wait()
-            loads[7].wait()
-            for turn in range(tiles):
+            if pieced:
+                swap_piece(0, 0).start()
+                mix_piece(0, core, 0)
+            for later in range(1, depths):
+                begin_trade(later)
+            for turn in range(tiles // 2, tiles):
                 for ref in range(3):
                     inverse(turn, ref, tile_starts[turn])
             for later in range(1, depths):
-                begin_gather(later)
-            for later in range(1, depths):
                 for ref in range(3):
                     phase_table(later, ref)
-            lag_table()
-            begin_last(0)
-            for turn in range(tiles // 2):
-                mix_tile(0, turn, tile_starts[turn])
-            swap_last(0).wait()
-            for turn in range(tiles // 2, tiles):
-                mix_tile(0, turn, tile_starts[turn])
+            if pieced:
+                mix_pieces(0, 1, sides)
             for later in range(1, depths):
-                begin_last(later)
+                begin_near_gather(later)
+            if pieced:
+                mix_pieces(0, sides, chips)
+                mix_last_piece(0)
+            else:
+                begin_last(0)
+                for turn in range(tiles // 2):
+                    mix_tile(0, turn, tile_starts[turn])
+                swap_last(0).wait()
+                for turn in range(tiles // 2, tiles):
+                    mix_tile(0, turn, tile_starts[turn])
         else:
             forward_y(0, fields.at[0])
             forward_y(1, fields.at[1])
             forward_x()
+            begin_near_last(d)
             for ref in range(3):
                 shift(d, ref)
             for turn in range(tiles):
@@ -472,6 +613,7 @@
                     swap_last(d).wait()
                 mix_tile(d, turn, tile_starts[turn])
         received[d, me] = cross[d, me]
+    lag_table()
     for d in range(depths):
         @pl.loop(1, devices)
         def _(hop):
@@ -512,7 +654,9 @@
             pltpu.VMEM(table_z.shape, jnp.bfloat16),
             pltpu.VMEM((rows_x, 4 * cols_y), jnp.bfloat16),
             pltpu.VMEM((rows_x, 4 * cols_y), jnp.float32),
-            pltpu.VMEM((depths, 3, 2, rows_x // 2 + chunk, cols_y), jnp.float32),
+            pltpu.VMEM((rows_x // 2 + strip, cols_y // 2), jnp.float32),
+            pltpu.VMEM((2, rows_x // 2 + strip, cols_y // 2), jnp.float32),
+            pltpu.VMEM((depths, 3, 2, rows_x // 2 + strip, cols_y), jnp.float32),
             pltpu.VMEM((3, rows_x, 4 * cols_y), jnp.bfloat16),
             pltpu.VMEM((tile, 4 * cols_y), jnp.bfloat16),
             pltpu.VMEM((rows_x // tile, 3, tile, 4 * cols_y), jnp.float32),
@@ -523,6 +667,7 @@
             pltpu.VMEM(held, jnp.bfloat16),
             pltpu.VMEM(held, jnp.bfloat16),
             pltpu.VMEM(held, jnp.bfloat16),
+            pltpu.VMEM((depths, 2, share_rows, cols_y), jnp.bfloat16),
             pltpu.VMEM((depths, share_rows, cols_y), jnp.bfloat16),
             pltpu.VMEM((depths, 2, chips, share_rows, cols_y), jnp.bfloat16),
             pltpu.VMEM((2 * devices, LAGS), jnp.float32),
@@ -530,6 +675,7 @@
             dma((depths, 4)),
             dma((depths, 2, chips)),
             dma((depths, 2, chips)),
+            dma((2, chips)),
             dma((depths, 2, devices)),
         ],
         cost_estimate=pl.CostEstimate(
@@ -549,18 +695,42 @@
     )
 
 
-def image_kernel(scale, crosses, weights, out):
-    _, slots, _, _, cols_y = crosses.shape
-    _, rows, _, _ = out.shape
-    step = pl.multiple_of(pl.program_id(1) * rows, rows)
-    values = crosses[pl.program_id(0), :, :, pl.ds(step, rows), :]
-    values = values.astype(jnp.float32).reshape(2 * slots, rows, cols_y)
-    values = jnp.swapaxes(values, 0, 1).astype(jnp.bfloat16)
-    for row in range(rows):
-        out[0, row] = scale * lax.dot_general(
-            values[row], weights[...], (((0,), (0,)), ((), ())),
-            preferred_element_type=jnp.float32,
-        )
+def image_kernel(scale, crosses, weights, out, held, sems):
+    depths, slots, _, rows, cols_y = crosses.shape
+    step = min(16, rows)
+    part = min(4, step)
+    count = depths * (rows // step)
+
+    def block(number, place):
+        d = number // (rows // step)
+        start = lax.rem(number, rows // step) * step + place * part
+        return d, pl.ds(start, part)
+
+    def write(number, place):
+        d, local = block(number, place)
+        return pltpu.make_async_copy(
+            held.at[d, local], out.at[d, local], sems.at[number, place]
+        )
+
+    @pl.loop(0, count)
+    def _(number):
+        d = number // (rows // step)
+        start = pl.multiple_of(lax.rem(number, rows // step) * step, step)
+        values = crosses[d, :, :, pl.ds(start, step), :]
+        values = values.astype(jnp.float32).reshape(2 * slots, step, cols_y)
+        values = jnp.swapaxes(values, 0, 1).astype(jnp.bfloat16)
+        for row in range(step):
+            held[d, start + row] = scale * lax.dot_general(
+                values[row], weights[...], (((0,), (0,)), ((), ())),
+                preferred_element_type=jnp.float32,
+            )
+            if row % part == part - 1:
+                write(number, row // part).start()
+
+    @pl.loop(0, count)
+    def _(number):
+        for place in range(step // part):
+            write(number, place).wait()
 
 
 def lag_image(crosses, weights):
@@ -568,13 +738,17 @@
     lag_count = weights.shape[1]
     step = min(16, rows)
     whole = pl.BlockSpec(memory_space=pltpu.VMEM)
+    image = (depths, rows, cols_y, lag_count)
     return pl.pallas_call(
         functools.partial(image_kernel, slots ** (-0.5)),
-        out_shape=jax.ShapeDtypeStruct((depths, rows, cols_y, lag_count), jnp.float32),
-        grid=(depths, rows // step),
+        out_shape=jax.ShapeDtypeStruct(image, jnp.float32),
         in_specs=[whole, whole],
-        out_specs=pl.BlockSpec((1, step, cols_y, lag_count), lambda d, r: (d, r, 0, 0)),
-        compiler_params=pltpu.CompilerParams(vmem_limit_bytes=24 * 1024 * 1024),
+        out_specs=pl.BlockSpec(memory_space=pltpu.HBM),
+        scratch_shapes=[
+            pltpu.VMEM(image, jnp.float32),
+            pltpu.SemaphoreType.DMA((depths * (rows // step), step // min(4, step))),
+        ],
+        compiler_params=pltpu.CompilerParams(vmem_limit_bytes=32 * 1024 * 1024),
     )(crosses, weights)
 
 

time: 51.8 us -> 50.5 us (0.975)
  Pallas kernels: 51.7 us -> 50.3 us
    pallas_call x1, Pallas kernels: 44.7 us -> 44 us  [cross_spectra(): pl.pallas_call(functools.partial(window_kernel, devices), out_shape=(jax....]
    pallas_call x1, Pallas kernels: 6.97 us -> 6.33 us  [lag_image(): pl.pallas_call(functools.partial(image_kernel, slots ** (-0.5)), out_shap...]
where the time goes in v5:
time: 50.5 us; the launch traced here: 50.3 us
  Pallas kernels  50.3 us (100%)
    pallas_call x1, Pallas kernels, cross_spectra(): pl.pallas_call(functools.partial(window_kernel, devices), out_shape=(jax....  44 us
    pallas_call x1, Pallas kernels, lag_image(): pl.pallas_call(functools.partial(image_kernel, slots ** (-0.5)), out_shap...  6.33 us

profile of v5, /device:TPU:0, one launch (start us, length us, event | category | flops | bytes accessed | tf_op | source)
XLA Modules:
  0.0 50.3 jit_solution(9129121256677239293)
XLA Ops:
  0.0 44.0 %shard_map.118 = (bf16[2,16,2,32,256]{4,3,2,1,0:T(8,128)(2,1)S(1)}, bf16[32,256]{1,0:T(8,128)(2,1)S(1)}) custom-call(s32[16]{0:T(128)} %bins.1, f32[2,3]{1,0:T(2,128)} %gaps.1, s32[2]{0:T(128)} %slab_map.1, s32[2]{0:T(128)} %corner.1, bf16[1,768,512]{2,1,0:T(8,128)(2,1)} %slab_in.1, bf16[2,512,256]{2,1,0:T(8,128)(2,1)} %bitcast.2, ...), custom_call_target="tpu_custom_call" | custom-call | flops 6442450944 | bytes 8388608 | tf_op jit(solution)/shard_map/pallas_call | solution.py:637
  44.0 6.3 %shard_map.119 = f32[2,32,256,256]{3,2,1,0:T(8,128)} custom-call(bf16[2,16,2,32,256]{4,3,2,1,0:T(8,128)(2,1)S(1)} %get-tuple-element.7.crosses, bf16[32,256]{1,0:T(8,128)(2,1)S(1)} %get-tuple-element.8.weights), custom_call_target="tpu_custom_call" | custom-call | tf_op jit(solution)/shard_map/pallas_call | solution.py:742

commit v6 on v5

--- a/solution.py
+++ b/solution.py
@@ -558,12 +558,12 @@
             loads[2].wait()
             forward_y(0, source)
             begin_scatter(0)
+            for later in range(1, depths):
+                begin_near_scatter(later)
             loads[3].wait()
             forward_y(1, receiver)
             loads[4].wait()
             forward_x()
-            for later in range(1, depths):
-                begin_near_scatter(later)
             for ref in range(3):
                 phase_table(0, ref)
                 shift(0, ref)
@@ -572,13 +572,13 @@
             for turn in range(tiles // 2):
                 for ref in range(3):
                     inverse(turn, ref, tile_starts[turn])
+            for later in range(1, depths):
+                begin_trade(later)
             begin_gather(0)
             loads[5].wait()
             if pieced:
                 swap_piece(0, 0).start()
                 mix_piece(0, core, 0)
-            for later in range(1, depths):
-                begin_trade(later)
             for turn in range(tiles // 2, tiles):
                 for ref in range(3):
                     inverse(turn, ref, tile_starts[turn])

time: 50.5 us -> 49.7 us (0.984)
  Pallas kernels: 50.3 us -> 49.5 us
    pallas_call x1, Pallas kernels: 44 us -> 43.2 us  [cross_spectra(): pl.pallas_call(functools.partial(window_kernel, devices), out_shape=(jax....]
where the time goes in v6:
time: 49.7 us; the launch traced here: 49.5 us
  Pallas kernels  49.5 us (100%)
    pallas_call x1, Pallas kernels, cross_spectra(): pl.pallas_call(functools.partial(window_kernel, devices), out_shape=(jax....  43.2 us
    pallas_call x1, Pallas kernels, lag_image(): pl.pallas_call(functools.partial(image_kernel, slots ** (-0.5)), out_shap...  6.32 us

profile of v6, /device:TPU:0, one launch (start us, length us, event | category | flops | bytes accessed | tf_op | source)
XLA Modules:
  0.0 49.5 jit_solution(17052991115172151576)
XLA Ops:
  0.0 43.2 %shard_map.118 = (bf16[2,16,2,32,256]{4,3,2,1,0:T(8,128)(2,1)S(1)}, bf16[32,256]{1,0:T(8,128)(2,1)S(1)}) custom-call(s32[16]{0:T(128)} %bins.1, f32[2,3]{1,0:T(2,128)} %gaps.1, s32[2]{0:T(128)} %slab_map.1, s32[2]{0:T(128)} %corner.1, bf16[1,768,512]{2,1,0:T(8,128)(2,1)} %slab_in.1, bf16[2,512,256]{2,1,0:T(8,128)(2,1)} %bitcast.2, ...), custom_call_target="tpu_custom_call" | custom-call | flops 6442450944 | bytes 8388608 | tf_op jit(solution)/shard_map/pallas_call | solution.py:637
  43.2 6.3 %shard_map.119 = f32[2,32,256,256]{3,2,1,0:T(8,128)} custom-call(bf16[2,16,2,32,256]{4,3,2,1,0:T(8,128)(2,1)S(1)} %get-tuple-element.7.crosses, bf16[32,256]{1,0:T(8,128)(2,1)S(1)} %get-tuple-element.8.weights), custom_call_target="tpu_custom_call" | custom-call | tf_op jit(solution)/shard_map/pallas_call | solution.py:742

commit v7 on v6

--- a/solution.py
+++ b/solution.py
@@ -287,6 +287,48 @@
                         piece * share_rows : (piece + 1) * share_rows
                     ]
 
+    half_y = cols_y // 2
+    unit = 0.5 * layer_thick
+    step_x = unit * 2.0 * math.pi / (rows_x * cell_width)
+    step_y = unit * 2.0 * math.pi / (cols_y * cell_width)
+    strips = middle // strip + 1
+    counted = lax.broadcasted_iota(jnp.int32, (strip, half_y), 0)
+    columns = lax.broadcasted_iota(jnp.int32, (strip, half_y), 1)
+
+    def strip_rows(number):
+        return pl.ds(pl.multiple_of(number * strip, strip), strip)
+
+    def reach_of(d, ref):
+        return angular * references[d][ref] * unit
+
+    def turn_of(reach, square):
+        radicand = reach * reach - square
+        size = jnp.abs(radicand)
+        depth = size * lax.rsqrt(jnp.maximum(size, 1e-30))
+        moving = radicand > 0.0
+        fading = jnp.exp(jnp.where(moving, 0.0, -2.0 * depth))
+        sine, cosine = sin_cos(jnp.where(moving, depth, 0.0) + (0.5 * math.pi - reach))
+        return fading * cosine, fading * sine
+
+    def fill_tables():
+        reach = jnp.zeros((strip, half_y), jnp.float32)
+        for d in range(depths):
+            for ref in range(3):
+                reach = jnp.where(columns == 3 * d + ref, reach_of(d, ref), reach)
+
+        @pl.loop(0, strips)
+        def _(number):
+            rows = strip_rows(number)
+            index = counted + number * strip
+            magnitude = jnp.where(index <= middle, index, index - middle)
+            wave_x = magnitude.astype(jnp.float32) * step_x
+            wave_y = columns.astype(jnp.float32) * step_y
+            squares[rows, :] = wave_x * wave_x + wave_y * wave_y
+            real, imag = turn_of(reach, wave_x * wave_x + (half_y * step_y) ** 2)
+            edge[0, rows, :] = real
+            edge[1, rows, :] = imag
+
+    fill_tables()
     loads[0].wait()
     for load in loads[1:]:
         load.start()
@@ -300,47 +342,6 @@
     pl.semaphore_wait(barrier, devices - 1)
     for d in range(depths):
         swap_first(d).start()
-
-    half_y = cols_y // 2
-    unit = 0.5 * layer_thick
-    step_x = unit * 2.0 * math.pi / (rows_x * cell_width)
-    step_y = unit * 2.0 * math.pi / (cols_y * cell_width)
-    strips = middle // strip + 1
-    counted = lax.broadcasted_iota(jnp.int32, (strip, half_y), 0)
-    columns = lax.broadcasted_iota(jnp.int32, (strip, half_y), 1)
-
-    def strip_rows(number):
-        return pl.ds(pl.multiple_of(number * strip, strip), strip)
-
-    def reach_of(d, ref):
-        return angular * references[d][ref] * unit
-
-    def turn_of(reach, square):
-        radicand = reach * reach - square
-        size = jnp.abs(radicand)
-        depth = size * lax.rsqrt(jnp.maximum(size, 1e-30))
-        moving = radicand > 0.0
-        fading = jnp.exp(jnp.where(moving, 0.0, -2.0 * depth))
-        sine, cosine = sin_cos(jnp.where(moving, depth, 0.0) + (0.5 * math.pi - reach))
-        return fading * cosine, fading * sine
-
-    def fill_tables():
-        reach = jnp.zeros((strip, half_y), jnp.float32)
-        for d in range(depths):
-            for ref in range(3):
-                reach = jnp.where(columns == 3 * d + ref, reach_of(d, ref), reach)
-
-        @pl.loop(0, strips)
-        def _(number):
-            rows = strip_rows(number)
-            index = counted + number * strip
-            magnitude = jnp.where(index <= middle, index, index - middle)
-            wave_x = magnitude.astype(jnp.float32) * step_x
-            wave_y = columns.astype(jnp.float32) * step_y
-            squares[rows, :] = wave_x * wave_x + wave_y * wave_y
-            real, imag = turn_of(reach, wave_x * wave_x + (half_y * step_y) ** 2)
-            edge[0, rows, :] = real
-            edge[1, rows, :] = imag
 
     def phase_table(d, ref):
         @pl.loop(0, strips)
@@ -553,11 +554,10 @@
             for turn in range(tiles)
         ]
         if d == 0:
-            fill_tables()
+            begin_scatter(0)
             loads[1].wait()
             loads[2].wait()
             forward_y(0, source)
-            begin_scatter(0)
             for later in range(1, depths):
                 begin_near_scatter(later)
             loads[3].wait()

time: 49.7 us -> 50.1 us (level)
  no operation moved by 1% of the time
where the time goes in v7:
time: 50.1 us; the launch traced here: 49.9 us
  Pallas kernels  49.9 us (100%)
    pallas_call x1, Pallas kernels, cross_spectra(): pl.pallas_call(functools.partial(window_kernel, devices), out_shape=(jax....  43.6 us
    pallas_call x1, Pallas kernels, lag_image(): pl.pallas_call(functools.partial(image_kernel, slots ** (-0.5)), out_shap...  6.32 us

profile of v7, /device:TPU:0, one launch (start us, length us, event | category | flops | bytes accessed | tf_op | source)
XLA Modules:
  0.0 49.9 jit_solution(12913786862128284436)
XLA Ops:
  0.0 43.6 %shard_map.118 = (bf16[2,16,2,32,256]{4,3,2,1,0:T(8,128)(2,1)S(1)}, bf16[32,256]{1,0:T(8,128)(2,1)S(1)}) custom-call(s32[16]{0:T(128)} %bins.1, f32[2,3]{1,0:T(2,128)} %gaps.1, s32[2]{0:T(128)} %slab_map.1, s32[2]{0:T(128)} %corner.1, bf16[1,768,512]{2,1,0:T(8,128)(2,1)} %slab_in.1, bf16[2,512,256]{2,1,0:T(8,128)(2,1)} %bitcast.2, ...), custom_call_target="tpu_custom_call" | custom-call | flops 6442450944 | bytes 8388608 | tf_op jit(solution)/shard_map/pallas_call | solution.py:637
  43.6 6.3 %shard_map.119 = f32[2,32,256,256]{3,2,1,0:T(8,128)} custom-call(bf16[2,16,2,32,256]{4,3,2,1,0:T(8,128)(2,1)S(1)} %get-tuple-element.7.crosses, bf16[32,256]{1,0:T(8,128)(2,1)S(1)} %get-tuple-element.8.weights), custom_call_target="tpu_custom_call" | custom-call | tf_op jit(solution)/shard_map/pallas_call | solution.py:742

commit v8 on v6

--- a/solution.py
+++ b/solution.py
@@ -553,11 +553,11 @@
             for turn in range(tiles)
         ]
         if d == 0:
+            begin_scatter(0)
             fill_tables()
             loads[1].wait()
             loads[2].wait()
             forward_y(0, source)
-            begin_scatter(0)
             for later in range(1, depths):
                 begin_near_scatter(later)
             loads[3].wait()

time: 49.7 us -> 50.1 us (level)
  no operation moved by 1% of the time
where the time goes in v8:
time: 50.1 us; the launch traced here: 49.9 us
  Pallas kernels  49.9 us (100%)
    pallas_call x1, Pallas kernels, cross_spectra(): pl.pallas_call(functools.partial(window_kernel, devices), out_shape=(jax....  43.6 us
    pallas_call x1, Pallas kernels, lag_image(): pl.pallas_call(functools.partial(image_kernel, slots ** (-0.5)), out_shap...  6.32 us

profile of v8, /device:TPU:0, one launch (start us, length us, event | category | flops | bytes accessed | tf_op | source)
XLA Modules:
  0.0 49.9 jit_solution(14574106351740681537)
XLA Ops:
  0.0 43.6 %shard_map.118 = (bf16[2,16,2,32,256]{4,3,2,1,0:T(8,128)(2,1)S(1)}, bf16[32,256]{1,0:T(8,128)(2,1)S(1)}) custom-call(s32[16]{0:T(128)} %bins.1, f32[2,3]{1,0:T(2,128)} %gaps.1, s32[2]{0:T(128)} %slab_map.1, s32[2]{0:T(128)} %corner.1, bf16[1,768,512]{2,1,0:T(8,128)(2,1)} %slab_in.1, bf16[2,512,256]{2,1,0:T(8,128)(2,1)} %bitcast.2, ...), custom_call_target="tpu_custom_call" | custom-call | flops 6442450944 | bytes 8388608 | tf_op jit(solution)/shard_map/pallas_call | solution.py:637
  43.6 6.3 %shard_map.119 = f32[2,32,256,256]{3,2,1,0:T(8,128)} custom-call(bf16[2,16,2,32,256]{4,3,2,1,0:T(8,128)(2,1)S(1)} %get-tuple-element.7.crosses, bf16[32,256]{1,0:T(8,128)(2,1)S(1)} %get-tuple-element.8.weights), custom_call_target="tpu_custom_call" | custom-call | tf_op jit(solution)/shard_map/pallas_call | solution.py:742
